TPU v7x, 32 devices: a whole 2x2x4 slice. The times are simulated.
32 devices in a mesh: gz: 4 (over y, x), phi: 8 (over z, core).
Axes of the slice: x: 2, y: 2, z: 4, core: 2. Of those that a mesh axis runs over, the one named last changes fastest.
Arguments:
- potential_in: float32 [256, 512, 256], P('phi', 'gz'), may hold values from -6 to 6
- charge: float32 [256, 512, 256], P('phi', 'gz'), may hold values from -6 to 6
- cell_kind: int32 [256, 512, 256], P('phi', 'gz'), may hold values from 0 to 2, as said below
Outputs:
- potential: float32 [256, 512, 256], P('phi', 'gz')
- shift_r: float32 [256, 512, 256], P('phi', 'gz')
- shift_rphi: float32 [256, 512, 256], P('phi', 'gz')
Inputs may be any that keep to these rules, and one draw needn't show every extreme that they name: `cell_kind`: 0 marks a free cell, 1 an electrode cell held at zero potential, 2 a boundary cell held at its given potential.
All inputs are finite; a program needn't handle non-finite values.
Results may differ from a plain program's by a relative error of at most 0.000073.
Values sent between devices are 32-bit elements; how exact they have to be, the bound alone decides.
A program may use at most 128 MiB of HBM per device.

v0:
```python
import functools
import math

import jax
import jax.numpy as jnp
import numpy as np
from jax import lax
from jax.experimental import pallas as pl
from jax.experimental.pallas import tpu as pltpu
from jax.sharding import PartitionSpec as P

PASSES = 3
HALVES = 2 * PASSES
RELAX = 1.5
FIXED = 1e30
MESH = pl.DeviceIdType.MESH
PAD = 8
LOAD_PAIRS = 2


def parity_mask(radial):
    row = lax.broadcasted_iota(jnp.int32, (8, radial), 0)
    lane = lax.broadcasted_iota(jnp.int32, (8, radial), 1)
    return (row + lane) % 2 == 0


def relax_kernel(
    slabs, rings, pot, chg, kind, coef, field, carry,
    pot_in, chg_in, kind_in, source, jsend, jrecv, zsend, zrecv, total, total_recv,
    load_sem, jsend_sem, jrecv_sem, zsend_sem, zrecv_sem, tsend_sem, trecv_sem,
):
    pairs = source.shape[1]
    depth = source.shape[2]
    radial = source.shape[3]
    half = depth // 2
    slab = lax.axis_index("gz")
    ring = lax.axis_index("phi")
    right, left = lax.rem(ring + 1, rings), lax.rem(ring + rings - 1, rings)

    chunks = [(0, 1), (pairs - 1, 1)]
    at = 1
    while at < pairs - 1:
        chunks.append((at, min(LOAD_PAIRS, pairs - 1 - at)))
        at += LOAD_PAIRS

    def loads(index):
        first, count = chunks[index]
        part = pl.ds(2 * first, 2 * count)
        return [
            pltpu.make_async_copy(src.at[part], dst.at[part], load_sem.at[index, n])
            for n, (src, dst) in enumerate(((pot, pot_in), (chg, chg_in), (kind, kind_in)))
        ]

    for index in range(len(chunks)):
        for copy in loads(index):
            copy.start()

    barrier = pltpu.get_barrier_semaphore()
    for neighbour in (left, right):
        pl.semaphore_signal(barrier, inc=1, device_id={"phi": neighbour}, device_id_type=MESH)
    for step in range(1, slabs):
        peer = lax.rem(slab + step, slabs)
        pl.semaphore_signal(barrier, inc=1, device_id={"gz": peer}, device_id_type=MESH)

    def prepare(pair):
        mask = parity_mask(radial)
        weight = coef[3]
        for row in range(0, depth, 8):
            rows = pl.ds(row, 8)
            out = pl.ds(row + PAD, 8)
            plane, charges = [], []
            for side in range(2):
                what = kind_in[2 * pair + side, rows, :]
                plane.append(jnp.where(what == 1, 0.0, pot_in[2 * pair + side, rows, :]))
                charges.append(
                    jnp.where(what == 0, weight * chg_in[2 * pair + side, rows, :], FIXED)
                )
            field[0, pair + 1, out, :] = jnp.where(mask, plane[0], plane[1])
            field[1, pair + 1, out, :] = jnp.where(mask, plane[1], plane[0])
            source[0, pair, rows, :] = jnp.where(mask, charges[0], charges[1])
            source[1, pair, rows, :] = jnp.where(mask, charges[1], charges[0])

    def jcopy(turn, side):
        return pltpu.make_async_remote_copy(
            src_ref=jsend.at[turn, side],
            dst_ref=jrecv.at[turn, side],
            send_sem=jsend_sem.at[turn, side],
            recv_sem=jrecv_sem.at[turn, side],
            device_id={"phi": (right, left)[side]},
            device_id_type=MESH,
        )

    def zcopy(turn, side):
        return pltpu.make_async_remote_copy(
            src_ref=zsend.at[turn, side],
            dst_ref=zrecv.at[turn, side],
            send_sem=zsend_sem.at[turn, side],
            recv_sem=zrecv_sem.at[turn, side],
            device_id={"gz": (lax.rem(slab + 1, slabs), lax.rem(slab + slabs - 1, slabs))[side]},
            device_id_type=MESH,
        )

    has_next, has_prev = slab < slabs - 1, slab > 0

    def send_j(turn, color, side):
        pair = (pairs, 1)[side]
        mask = parity_mask(radial)
        first = (color == 1) == (side == 0)
        for row in range(0, half, 8):
            upper = field[color, pair, pl.ds(PAD + row, 8), :]
            lower = pltpu.roll(field[color, pair, pl.ds(PAD + row + half, 8), :], 1, axis=1)
            jsend[turn, side, pl.ds(row, 8), :] = (
                jnp.where(mask, upper, lower) if first else jnp.where(mask, lower, upper)
            )
        jcopy(turn, side).start()

    def take_j(turn, color, side):
        jcopy(turn, side).wait_recv()
        pair = (0, pairs + 1)[side]
        for row in range(0, half, 8):
            face = jrecv[turn, side, pl.ds(row, 8), :]
            field[color, pair, pl.ds(PAD + row, 8), :] = face
            field[color, pair, pl.ds(PAD + row + half, 8), :] = pltpu.roll(face, radial - 1, axis=1)

    def send_z(turn, color):
        for pair in range(pairs):
            zsend[turn, 0, pair] = field[color, pair + 1, pl.ds(PAD + depth - 1, 1), :]
            zsend[turn, 1, pair] = field[color, pair + 1, pl.ds(PAD, 1), :]

        @pl.when(has_next)
        def _():
            zcopy(turn, 0).start()

        @pl.when(has_prev)
        def _():
            zcopy(turn, 1).start()

    def take_z(turn, color):
        @pl.when(has_prev)
        def _():
            zcopy(turn, 0).wait_recv()
            for pair in range(pairs):
                field[color, pair + 1, pl.ds(PAD - 1, 1), :] = zrecv[turn, 0, pair]

        @pl.when(has_next)
        def _():
            zcopy(turn, 1).wait_recv()
            for pair in range(pairs):
                field[color, pair + 1, pl.ds(PAD + depth, 1), :] = zrecv[turn, 1, pair]

    def update(pair, color, blocks):
        other = 1 - color
        mask = parity_mask(radial)
        out_c, in_c, around_c, z_c = coef[0], coef[1], coef[2], coef[3]
        before, after = (pair - 1, pair + 1) if color == 0 else (pair + 1, pair - 1)
        for row in blocks:
            rows = pl.ds(row + PAD, 8)
            own = field[color, pair, rows, :]
            near = field[other, pair, rows, :]
            beside = near + jnp.where(mask, field[other, before, rows, :], field[other, after, rows, :])
            along = (
                field[other, pair, pl.ds(row + PAD - 1, 8), :]
                + field[other, pair, pl.ds(row + PAD + 1, 8), :]
            )
            put = source[color, pair - 1, pl.ds(row, 8), :]
            fresh = (
                put
                - (RELAX - 1.0) * own
                + out_c * pltpu.roll(near, radial - 1, axis=1)
                + in_c * pltpu.roll(near, 1, axis=1)
                + around_c * beside
                + z_c * along
            )
            field[color, pair, rows, :] = jnp.where(put < 0.5 * FIXED, fresh, own)

    edge = jnp.zeros((PAD, radial), jnp.float32)
    for color in range(2):
        for pair in range(1, pairs + 1):
            field[color, pair, pl.ds(0, PAD), :] = edge
            field[color, pair, pl.ds(PAD + depth, PAD), :] = edge

    for index in range(2):
        for copy in loads(index):
            copy.wait()
        prepare(chunks[index][0])
    pl.semaphore_wait(barrier, 2 + slabs - 1)
    for side in range(2):
        send_j(0, 1, side)
    for index in range(2, len(chunks)):
        for copy in loads(index):
            copy.wait()
        first, count = chunks[index]
        lax.fori_loop(first, first + count, lambda a, _: (prepare(a), 0)[1], 0)
    send_z(0, 1)

    whole, ends, inner = range(0, depth, 8), (0, depth - 8), range(8, depth - 8, 8)
    for turn in range(HALVES):
        color = turn % 2
        take_z(turn, 1 - color)
        for side in range(2):
            take_j(turn, 1 - color, side)
            update((1, pairs)[side], color, whole)
            send_j(turn + 1, color, 1 - side)
        if turn + 1 < HALVES:
            lax.fori_loop(2, pairs, lambda a, _: (update(a, color, ends), 0)[1], 0)
            send_z(turn + 1, color)
            lax.fori_loop(2, pairs, lambda a, _: (update(a, color, inner), 0)[1], 0)
        else:
            lax.fori_loop(2, pairs, lambda a, _: (update(a, color, whole), 0)[1], 0)

    def sum_up(pair):
        mask = parity_mask(radial)
        even = jnp.zeros((8, radial), jnp.float32)
        odd = jnp.zeros((8, radial), jnp.float32)
        for row in range(0, depth, 8):
            red = field[0, pair, pl.ds(row + PAD, 8), :]
            black = field[1, pair, pl.ds(row + PAD, 8), :]
            even += jnp.where(mask, red, black)
            odd += jnp.where(mask, black, red)
        total[pair, pl.ds(0, 1), :] = jnp.sum(even, axis=0, keepdims=True)
        total[pair, pl.ds(1, 1), :] = jnp.sum(odd, axis=0, keepdims=True)

    lax.fori_loop(1, pairs + 1, lambda a, _: (sum_up(a), 0)[1], 0)
    for side in range(2):
        take_j(HALVES, 1, side)
    sum_up(0)
    sum_up(pairs + 1)

    def tcopy(step):
        return pltpu.make_async_remote_copy(
            src_ref=total,
            dst_ref=total_recv.at[step - 1],
            send_sem=tsend_sem.at[step - 1],
            recv_sem=trecv_sem.at[step - 1],
            device_id={"gz": lax.rem(slab + step, slabs)},
            device_id_type=MESH,
        )

    for step in range(1, slabs):
        tcopy(step).start()
    beyond = jnp.zeros(carry.shape, jnp.float32)
    for step in range(1, slabs):
        tcopy(step).wait_recv()
        beyond = beyond + jnp.where(step > slab, total_recv[step - 1], 0.0)
    carry[...] = beyond

    for step in range(1, slabs):
        tcopy(step).wait_send()
    for turn in range(HALVES + 1):
        for side in range(2):
            jcopy(turn, side).wait_send()
    for turn in range(HALVES):
        @pl.when(has_next)
        def _():
            zcopy(turn, 0).wait_send()

        @pl.when(has_prev)
        def _():
            zcopy(turn, 1).wait_send()


def drift_kernel(coef, field, carry, potential, shift_r, shift_phi, sums):
    step = pl.program_id(0)
    depth, radial = potential.shape[1], potential.shape[2]
    mask = parity_mask(radial)
    row = lax.broadcasted_iota(jnp.int32, (8, radial), 0)
    slot = lax.rem(step, 3)
    runs = [jnp.broadcast_to(carry[0, pl.ds(side, 1), :], (8, radial)) for side in range(2)]
    for at in range(depth - 8, -8, -8):
        red = field[0, 0, pl.ds(at + PAD, 8), :]
        black = field[1, 0, pl.ds(at + PAD, 8), :]
        for side in range(2):
            part = jnp.where(mask, red, black) if side == 0 else jnp.where(mask, black, red)
            for hop in (1, 2, 4):
                part = part + jnp.where(row < 8 - hop, pltpu.roll(part, 8 - hop, axis=0), 0.0)
            sums[slot, side, pl.ds(at, 8), :] = part + runs[side]
            runs[side] = runs[side] + jnp.broadcast_to(part[0:1, :], (8, radial))

    @pl.when(step >= 2)
    def _():
        mid, low = lax.rem(step + 2, 3), lax.rem(step + 1, 3)
        out_c, in_c, phi_c = coef[4], coef[5], coef[6]
        for at in range(0, depth, 8):
            rows = pl.ds(at, 8)
            planes = (sums[low, 1, rows, :], sums[mid, 0, rows, :], sums[mid, 1, rows, :], sums[slot, 0, rows, :])
            for side in range(2):
                here = planes[side + 1]
                along_r = out_c * pltpu.roll(here, radial - 1, axis=1) + in_c * pltpu.roll(here, 1, axis=1)
                along_phi = phi_c * (planes[side + 2] - planes[side])
                shift_r[side, rows, :] = along_r + 0.3 * along_phi
                shift_phi[side, rows, :] = along_phi - 0.3 * along_r


def coefficients(radial, sectors):
    radius = radial * 0.5 + np.arange(radial, dtype=np.float64) + 0.5
    step_phi = 2.0 * math.pi / sectors
    around = 1.0 / (radius * step_phi) ** 2
    diag = 4.0 + 2.0 * around
    has_next = np.arange(radial) < radial - 1
    has_prev = np.arange(radial) > 0
    drift = 1.0 / (1.09 * 32.0)
    rows = [
        RELAX * (1.0 + 0.5 / radius) / diag * has_next,
        RELAX * (1.0 - 0.5 / radius) / diag * has_prev,
        RELAX * around / diag,
        RELAX / diag,
        -0.5 * drift * has_next,
        0.5 * drift * has_prev,
        -0.5 * drift / (radius * step_phi),
        np.zeros(radial),
    ]
    stacked = np.stack(rows).astype(np.float32)
    return jnp.asarray(np.ascontiguousarray(np.broadcast_to(stacked[:, None, :], (8, 8, radial))))


def local(slabs, rings, potential_in, charge, cell_kind):
    sectors, depth, radial = potential_in.shape
    pairs = sectors // 2
    tall = depth + 2 * PAD
    coef = coefficients(radial, sectors * rings)
    any_spec = pl.BlockSpec(memory_space=pl.ANY)
    vmem_spec = pl.BlockSpec(memory_space=pltpu.VMEM)
    chunks = 2 + -(-(pairs - 2) // LOAD_PAIRS)
    f32 = jnp.float32
    field, carry = pl.pallas_call(
        functools.partial(relax_kernel, slabs, rings),
        out_shape=(
            jax.ShapeDtypeStruct((2, pairs + 2, tall, radial), f32),
            jax.ShapeDtypeStruct((pairs + 2, 2, radial), f32),
        ),
        in_specs=[any_spec, any_spec, any_spec, vmem_spec],
        out_specs=(vmem_spec, vmem_spec),
        scratch_shapes=[
            pltpu.VMEM((sectors, depth, radial), f32),
            pltpu.VMEM((sectors, depth, radial), f32),
            pltpu.VMEM((sectors, depth, radial), jnp.int32),
            pltpu.VMEM((2, pairs, depth, radial), f32),
            pltpu.VMEM((HALVES + 1, 2, depth // 2, radial), f32),
            pltpu.VMEM((HALVES + 1, 2, depth // 2, radial), f32),
            pltpu.VMEM((HALVES, 2, pairs, 1, radial), f32),
            pltpu.VMEM((HALVES, 2, pairs, 1, radial), f32),
            pltpu.VMEM((pairs + 2, 2, radial), f32),
            pltpu.VMEM((slabs - 1, pairs + 2, 2, radial), f32),
            pltpu.SemaphoreType.DMA((chunks, 3)),
            pltpu.SemaphoreType.DMA((HALVES + 1, 2)),
            pltpu.SemaphoreType.DMA((HALVES + 1, 2)),
            pltpu.SemaphoreType.DMA((HALVES, 2)),
            pltpu.SemaphoreType.DMA((HALVES, 2)),
            pltpu.SemaphoreType.DMA((slabs - 1,)),
            pltpu.SemaphoreType.DMA((slabs - 1,)),
        ],
        compiler_params=pltpu.CompilerParams(collective_id=0, has_side_effects=True),
    )(potential_in, charge, cell_kind, coef)

    block = jax.ShapeDtypeStruct((sectors, depth, radial), f32)

    def out_map(g):
        return (jnp.maximum(g - 2, 0), 0, 0)

    return pl.pallas_call(
        drift_body,
        out_shape=(block, block, block),
        grid=(pairs + 2,),
        in_specs=[
            pl.BlockSpec((8, 8, radial), lambda g: (0, 0, 0)),
            pl.BlockSpec((2, 1, tall, radial), lambda g: (0, g, 0, 0)),
            pl.BlockSpec((1, 2, radial), lambda g: (g, 0, 0)),
        ],
        out_specs=(pl.BlockSpec((2, depth, radial), lambda g: (jnp.clip(g - 1, 0, pairs - 1), 0, 0)),)
        + (pl.BlockSpec((2, depth, radial), out_map),) * 2,
        scratch_shapes=[pltpu.VMEM((3, 2, depth, radial), f32)],
    )(coef, field, carry)


def drift_body(coef, field, carry, potential, shift_r, shift_phi, sums):
    step = pl.program_id(0)
    depth, radial = potential.shape[1], potential.shape[2]

    @pl.when(jnp.logical_and(step >= 1, step < pl.num_programs(0) - 1))
    def _():
        mask = parity_mask(radial)
        for at in range(0, depth, 8):
            red = field[0, 0, pl.ds(at + PAD, 8), :]
            black = field[1, 0, pl.ds(at + PAD, 8), :]
            potential[0, pl.ds(at, 8), :] = jnp.where(mask, red, black)
            potential[1, pl.ds(at, 8), :] = jnp.where(mask, black, red)

    drift_kernel(coef, field, carry, potential, shift_r, shift_phi, sums)


def solution(mesh):
    spec = P("phi", "gz", None)
    body = functools.partial(local, mesh.shape["gz"], mesh.shape["phi"])
    return jax.shard_map(body, mesh=mesh, in_specs=(spec,) * 3, out_specs=(spec,) * 3, check_vma=False)
```

profile of v0, /device:TPU:0, one launch (start us, length us, event | category | flops | bytes accessed | tf_op | source)
XLA Modules:
  0.0 61.8 jit_solution(13456183018384340223)
XLA Ops:
  0.6 45.9 %shard_map.67 = (f32[2,18,144,256]{3,2,1,0:T(8,128)}, f32[18,2,256]{2,1,0:T(2,128)}) custom-call(f32[32,128,256]{2,1,0:T(8,128)} %pot.1, f32[32,128,256]{2,1,0:T(8,128)} %chg.1, s32[32,128,256]{2,1,0:T(8,128)} %kind.1, f32[8,8,256]{2,1,0:T(8,128)} %constant.2.clone.coef), custom_call_target="tpu_custom_call" | custom-call | tf_op jit(solution)/shard_map/pallas_call | solution.py:325
  46.5 15.2 %shard_map.68 = (f32[32,128,256]{2,1,0:T(8,128)}, f32[32,128,256]{2,1,0:T(8,128)}, f32[32,128,256]{2,1,0:T(8,128)}) custom-call(f32[8,8,256]{2,1,0:T(8,128)} %constant.2.clone.coef, f32[2,18,144,256]{3,2,1,0:T(8,128)} %get-tuple-element.5.field, f32[18,2,256]{2,1,0:T(2,128)} %get-tuple-element.6.carry), custom_call_target="tpu_custom_call" | custom-call | tf_op jit(solution)/shard_map/pallas_call | solution.py:360
where the time goes:
time: 62.3 us; the launch traced here: 61.8 us
  Pallas kernels  61.1 us (98%)
  between operations  0.64 us (1%)
    pallas_call x1, Pallas kernels, local(): pl.pallas_call(functools.partial(relax_kernel, slabs, rings), out_shape=(...  45.9 us
    pallas_call x1, Pallas kernels, local(): pl.pallas_call(drift_body, out_shape=(block, block, block), grid=(pairs +...  15.2 us

commit v1 on v0

v1 whole, which is shorter than its diff:
```python
import functools
import math

import jax
import jax.numpy as jnp
import numpy as np
from jax import lax
from jax.experimental import pallas as pl
from jax.experimental.pallas import tpu as pltpu
from jax.sharding import PartitionSpec as P

PASSES = 3
RELAX = 1.5
FIXED = 1e30
MESH = pl.DeviceIdType.MESH
PAD = 16
LANES = 128
RED, BLACK = 0, 1


def parity_mask():
    row = lax.broadcasted_iota(jnp.int32, (8, LANES), 0)
    lane = lax.broadcasted_iota(jnp.int32, (8, LANES), 1)
    return (row + lane) % 2 == 0


def beside(halves, lane):
    ahead = [pltpu.roll(x, LANES - 1, axis=1) for x in halves]
    behind = [pltpu.roll(x, 1, axis=1) for x in halves]
    last = len(halves) - 1
    outer = [ahead[h] if h == last else jnp.where(lane == LANES - 1, ahead[h + 1], ahead[h]) for h in range(last + 1)]
    inner = [behind[h] if h == 0 else jnp.where(lane == 0, behind[h - 1], behind[h]) for h in range(last + 1)]
    return outer, inner


def relax_kernel(
    slabs, rings, pot, chg, kind, coef, full, carry,
    pot_in, chg_in, kind_in, red, black, source, zsend, zrecv, crecv, total, total_recv, edge, edge_recv,
    load_sem, jsend_sem, jrecv_sem, zsend_sem, zrecv_sem, csend_sem, crecv_sem,
    fsend_sem, frecv_sem, tsend_sem, trecv_sem, esend_sem, erecv_sem,
):
    halves = red.shape[0]
    sectors, depth, radial = pot_in.shape
    pairs = sectors // 2
    tiles = depth // 8
    slab = lax.axis_index("gz")
    ring = lax.axis_index("phi")
    right, left = lax.rem(ring + 1, rings), lax.rem(ring + rings - 1, rings)
    has_next, has_prev = slab < slabs - 1, slab > 0
    whole_rows = pl.ds(PAD, depth)
    halo = (pairs, pairs + 1)

    def loads(slot, planes, rows):
        return [
            pltpu.make_async_copy(src.at[planes, rows], dst.at[planes, rows], load_sem.at[slot, n])
            for n, (src, dst) in enumerate(((pot, pot_in), (chg, chg_in), (kind, kind_in)))
        ]

    every, middle = pl.ds(0, sectors), pl.ds(8, depth - 16)
    ends = [loads(pairs, every, pl.ds(0, 8)), loads(pairs + 1, every, pl.ds(depth - 8, 8))]

    def pair_loads(p):
        return loads(p, pl.ds(2 * p, 2), middle)

    for batch in ends:
        for copy in batch:
            copy.start()
    for p in (0, pairs - 1):
        for copy in pair_loads(p):
            copy.start()

    def start_pair(p, _):
        for copy in pair_loads(p):
            copy.start()
        return 0

    lax.fori_loop(1, pairs - 1, start_pair, 0)

    barrier = pltpu.get_barrier_semaphore()
    for neighbour in (left, right):
        pl.semaphore_signal(barrier, inc=1, device_id={"phi": neighbour}, device_id_type=MESH)
    for step in range(1, slabs):
        peer = lax.rem(slab + step, slabs)
        for column in (left, ring, right):
            pl.semaphore_signal(barrier, inc=1, device_id={"gz": peer, "phi": column}, device_id_type=MESH)

    nothing = jnp.zeros((8, LANES), jnp.float32)
    held = jnp.full((8, LANES), FIXED, jnp.float32)
    for h in range(halves):
        for rows in (pl.ds(PAD - 8, 8), pl.ds(PAD + depth, 8)):
            for p in range(black.shape[1]):
                black[h, p, rows, :] = nothing
            for p in range(pairs):
                red[h, p, rows, :] = nothing
                source[RED, h, p, rows, :] = held

    def prepare(p, which):
        mask = parity_mask()
        for tile in which:
            rows, out = pl.ds(8 * tile, 8), pl.ds(PAD + 8 * tile, 8)
            for h in range(halves):
                lanes = pl.ds(LANES * h, LANES)
                plane, charges = [], []
                for side in range(2):
                    what = kind_in[2 * p + side, rows, lanes]
                    plane.append(jnp.where(what == 1, 0.0, pot_in[2 * p + side, rows, lanes]))
                    charges.append(jnp.where(what == 0, chg_in[2 * p + side, rows, lanes], FIXED))
                red[h, p, out, :] = jnp.where(mask, plane[0], plane[1])
                black[h, p, out, :] = jnp.where(mask, plane[1], plane[0])
                source[RED, h, p, out, :] = jnp.where(mask, charges[0], charges[1])
                source[BLACK, h, p, out, :] = jnp.where(mask, charges[1], charges[0])

    def fresh_tile(color, p, near, before, after, tile):
        own, other = (red, black) if color == RED else (black, red)
        mask = parity_mask()
        lane = lax.broadcasted_iota(jnp.int32, (8, LANES), 1)
        first, second = (before, after) if color == RED else (after, before)
        at = PAD + 8 * tile
        rows = pl.ds(at, 8)
        here = [other[h, near, rows, :] for h in range(halves)]
        outer, inner = beside(here, lane)
        result = []
        for h in range(halves):
            around = here[h] + jnp.where(mask, other[h, first, rows, :], other[h, second, rows, :])
            along = other[h, near, pl.ds(at - 1, 8), :] + other[h, near, pl.ds(at + 1, 8), :]
            put = source[color, h, p, rows, :]
            old = own[h, p, rows, :]
            gathered = (put + along) + (coef[0, h] * outer[h] + coef[1, h] * inner[h]) + coef[2, h] * around
            fresh = coef[3, h] * gathered - (RELAX - 1.0) * old
            result.append((jnp.where(put < 0.5 * FIXED, fresh, old), here[h]))
        return result

    def update(color, p, near, before, after, which):
        own = red if color == RED else black
        for tile in which:
            for h, (value, _) in enumerate(fresh_tile(color, p, near, before, after, tile)):
                own[h, p, pl.ds(PAD + 8 * tile, 8), :] = value

    def halo_black(exchange):
        return pairs + 2 * exchange, pairs + 2 * exchange + 1

    def jcopies(exchange, side):
        edge_pair = (pairs - 1, 0)[side]
        moves = [(black, (slice(None), edge_pair), (slice(None), halo_black(exchange)[side]))]
        if exchange == 0:
            moves.append((red, (slice(None), edge_pair), (slice(None), halo[side])))
            moves.append((source, (RED, slice(None), edge_pair), (RED, slice(None), halo[side])))
        return [
            pltpu.make_async_remote_copy(
                src_ref=ref.at[(*src, whole_rows)],
                dst_ref=ref.at[(*dst, whole_rows)],
                send_sem=jsend_sem.at[exchange, n, side],
                recv_sem=jrecv_sem.at[exchange, n, side],
                device_id={"phi": (right, left)[side]},
                device_id_type=MESH,
            )
            for n, (ref, src, dst) in enumerate(moves)
        ]

    slots = (lambda exchange: (0, PASSES) if exchange == 0 else (exchange,))

    def zcopy(slot, side):
        return pltpu.make_async_remote_copy(
            src_ref=zsend.at[slot, side],
            dst_ref=zrecv.at[slot, side],
            send_sem=zsend_sem.at[slot, side],
            recv_sem=zrecv_sem.at[slot, side],
            device_id={"gz": (lax.rem(slab + 1, slabs), lax.rem(slab + slabs - 1, slabs))[side]},
            device_id_type=MESH,
        )

    def ccopy(exchange, side, face):
        return pltpu.make_async_remote_copy(
            src_ref=zsend.at[exchange, side, :, (pairs - 1, 0)[face]],
            dst_ref=crecv.at[exchange, side, face],
            send_sem=csend_sem.at[exchange, side, face],
            recv_sem=crecv_sem.at[exchange, side, face],
            device_id={
                "gz": (lax.rem(slab + 1, slabs), lax.rem(slab + slabs - 1, slabs))[side],
                "phi": (right, left)[face],
            },
            device_id_type=MESH,
        )

    def zmoves(exchange, side):
        return [zcopy(slot, side) for slot in slots(exchange)] + [ccopy(exchange, side, face) for face in range(2)]

    def when_sides(exchange, gate, act):
        for side in range(2):
            @pl.when(gate[side])
            def _():
                for copy in zmoves(exchange, side):
                    act(copy)

    def send_z(exchange):
        for h in range(halves):
            for p in range(pairs):
                zsend[exchange, 0, h, p] = black[h, p, pl.ds(PAD + depth - 2, 2), :]
                zsend[exchange, 1, h, p] = black[h, p, pl.ds(PAD, 2), :]
                if exchange == 0:
                    for side, at in ((0, PAD + depth - 1), (1, PAD)):
                        zsend[PASSES, side, h, p, pl.ds(0, 1), :] = red[h, p, pl.ds(at, 1), :]
                        zsend[PASSES, side, h, p, pl.ds(1, 1), :] = source[RED, h, p, pl.ds(at, 1), :]

    def start_z(exchange):
        when_sides(exchange, (has_next, has_prev), lambda copy: copy.start())

    def take_z(exchange):
        for side in range(2):
            @pl.when((has_prev, has_next)[side])
            def _():
                for copy in zmoves(exchange, side):
                    copy.wait_recv()
                two = pl.ds((PAD - 2, PAD + depth)[side], 2)
                one = pl.ds((PAD - 1, PAD + depth)[side], 1)
                for h in range(halves):
                    for p in range(pairs):
                        black[h, p, two, :] = zrecv[exchange, side, h, p]
                        if exchange == 0:
                            red[h, p, one, :] = zrecv[PASSES, side, h, p, pl.ds(0, 1), :]
                            source[RED, h, p, one, :] = zrecv[PASSES, side, h, p, pl.ds(1, 1), :]
                    for face in range(2):
                        black[h, halo_black(exchange)[face], two, :] = crecv[exchange, side, face, h]

    def start_j(exchange):
        for side in range(2):
            for copy in jcopies(exchange, side):
                copy.start()

    def loop(low, high, body):
        lax.fori_loop(low, high, lambda p, _: (body(p), 0)[1], 0)

    inside = range(1, tiles - 1)
    whole = range(tiles)
    rims = (0, tiles - 1)

    def red_inside(p):
        update(RED, p, p, p - 1, p + 1, inside)

    def red_edges(exchange):
        low, high = halo_black(exchange)
        take_z(exchange)
        loop(1, pairs - 1, lambda p: update(RED, p, p, p - 1, p + 1, (-1, 0, tiles - 1, tiles)))
        for side in range(2):
            for copy in jcopies(exchange, side):
                copy.wait_recv()
            if exchange == 0:
                for copy in jcopies(exchange, 1 - side):
                    copy.wait_send()
        for side in range(2):
            p, before, after = ((0, low, 1), (pairs - 1, pairs - 2, high))[side]
            update(RED, p, p, before, after, range(-1, tiles + 1))
            p, near, before, after = ((halo[0], low, low, 0), (halo[1], high, pairs - 1, high))[side]
            update(RED, p, near, before, after, whole)

    for batch in ends:
        for copy in batch:
            copy.wait()
    loop(0, pairs, lambda p: prepare(p, rims))
    send_z(0)
    pl.semaphore_wait(barrier, 2 + 3 * (slabs - 1))
    start_z(0)
    for p in (0, pairs - 1):
        for copy in pair_loads(p):
            copy.wait()
        prepare(p, inside)
    start_j(0)

    def arrive(p):
        for copy in pair_loads(p):
            copy.wait()
        prepare(p, inside)

    arrive(1)

    def arrive_and_update(p):
        arrive(p)
        red_inside(p - 1)

    loop(2, pairs - 1, arrive_and_update)
    red_inside(pairs - 2)

    for sweep in range(PASSES):
        if sweep > 0:
            loop(1, pairs - 1, red_inside)
        red_edges(sweep)
        if sweep > 0:
            for side in range(2):
                for copy in jcopies(sweep, side):
                    copy.wait_send()
        if sweep < PASSES - 1:
            update(BLACK, 0, 0, halo[0], 1, whole)
            update(BLACK, pairs - 1, pairs - 1, pairs - 2, halo[1], whole)
            start_j(sweep + 1)
            loop(1, pairs - 1, lambda p: update(BLACK, p, p, p - 1, p + 1, rims))
            send_z(sweep + 1)
            start_z(sweep + 1)
            loop(1, pairs - 1, lambda p: update(BLACK, p, p, p - 1, p + 1, inside))

    def finish(p, before, after):
        mask = parity_mask()
        sums = [[jnp.zeros((8, LANES), jnp.float32) for _ in range(2)] for _ in range(halves)]
        for tile in whole:
            rows = pl.ds(8 * tile, 8)
            for h, (value, near) in enumerate(fresh_tile(BLACK, p, p, before, after, tile)):
                for side in range(2):
                    plane = jnp.where(mask, near, value) if side == 0 else jnp.where(mask, value, near)
                    full[2 * p + 1 + side, rows, pl.ds(LANES * h, LANES)] = plane
                    sums[h][side] = sums[h][side] + plane
        for h in range(halves):
            for side in range(2):
                total[h, pl.ds(2 * p + side, 1), :] = jnp.sum(sums[h][side], axis=0, keepdims=True)

    def fcopy(side):
        return pltpu.make_async_remote_copy(
            src_ref=full.at[(sectors, 1)[side]],
            dst_ref=full.at[(0, sectors + 1)[side]],
            send_sem=fsend_sem.at[side],
            recv_sem=frecv_sem.at[side],
            device_id={"phi": (right, left)[side]},
            device_id_type=MESH,
        )

    finish(0, halo[0], 1)
    finish(pairs - 1, pairs - 2, halo[1])
    for side in range(2):
        fcopy(side).start()
    loop(1, pairs - 1, lambda p: finish(p, p - 1, p + 1))
    for h in range(halves):
        edge[0, h] = total[h, pl.ds(sectors - 1, 1), :]
        edge[1, h] = total[h, pl.ds(0, 1), :]

    def tcopies(step):
        lower = lax.rem(slab + slabs - step, slabs)
        return [
            pltpu.make_async_remote_copy(
                src_ref=total,
                dst_ref=total_recv.at[step - 1],
                send_sem=tsend_sem.at[step - 1],
                recv_sem=trecv_sem.at[step - 1],
                device_id={"gz": lower},
                device_id_type=MESH,
            )
        ] + [
            pltpu.make_async_remote_copy(
                src_ref=edge.at[face],
                dst_ref=edge_recv.at[step - 1, face],
                send_sem=esend_sem.at[step - 1, face],
                recv_sem=erecv_sem.at[step - 1, face],
                device_id={"gz": lower, "phi": (right, left)[face]},
                device_id_type=MESH,
            )
            for face in range(2)
        ]

    for step in range(1, slabs):
        @pl.when(slab >= step)
        def _():
            for copy in tcopies(step):
                copy.start()

    carry[...] = jnp.zeros(carry.shape, jnp.float32)
    for step in range(1, slabs):
        @pl.when(slab + step < slabs)
        def _():
            for copy in tcopies(step):
                copy.wait_recv()
            for h in range(halves):
                carry[h, pl.ds(1, sectors), :] = carry[h, pl.ds(1, sectors), :] + total_recv[step - 1, h]
                for face, at in ((0, 0), (1, sectors + 1)):
                    carry[h, pl.ds(at, 1), :] = carry[h, pl.ds(at, 1), :] + edge_recv[step - 1, face, h]

    for side in range(2):
        fcopy(side).wait_recv()
        fcopy(side).wait_send()
    for step in range(1, slabs):
        @pl.when(slab >= step)
        def _():
            for copy in tcopies(step):
                copy.wait_send()
    for sweep in range(PASSES):
        when_sides(sweep, (has_next, has_prev), lambda copy: copy.wait_send())


def drift_kernel(
    coef, full, carry, potential, shift_r, shift_phi,
    runs, ones, twos, sums, out_r, out_phi, pot_sem, out_sem,
):
    halves, tall = runs.shape[0], runs.shape[1]
    sectors = full.shape[0] - 2
    depth = full.shape[1]
    pairs = sectors // 2
    tiles = depth // 8
    row = lax.broadcasted_iota(jnp.int32, (8, LANES), 0)
    lane = lax.broadcasted_iota(jnp.int32, (8, LANES), 1)

    parts = pot_sem.shape[0]

    def pot_copy(part):
        count = sectors // parts
        return pltpu.make_async_copy(
            full.at[pl.ds(1 + part * count, count)], potential.at[pl.ds(part * count, count)], pot_sem.at[part]
        )

    def out_copies(pair, slot):
        planes = pl.ds(2 * pair, 2)
        return [
            pltpu.make_async_copy(out_r.at[slot], shift_r.at[planes], out_sem.at[slot, 0]),
            pltpu.make_async_copy(out_phi.at[slot], shift_phi.at[planes], out_sem.at[slot, 1]),
        ]

    for part in range(parts):
        pot_copy(part).start()

    def integrate(plane, slot):
        for h in range(halves):
            after = jnp.broadcast_to(carry[h, pl.ds(plane, 1), :], (8, LANES))
            run = jnp.where(row == 0, after, 0.0)
            for ref in (runs, ones, twos):
                ref[h, pl.ds(depth, 8), :] = run
            for tile in range(tiles - 1, -1, -1):
                run = run + full[plane, pl.ds(8 * tile, 8), pl.ds(LANES * h, LANES)]
                runs[h, pl.ds(8 * tile, 8), :] = run
        for h in range(halves):
            for src, dst, hop in ((runs, ones, 1), (ones, twos, 2)):
                for tile in range(tiles - 1, -1, -1):
                    at = 8 * tile
                    dst[h, pl.ds(at, 8), :] = src[h, pl.ds(at, 8), :] + src[h, pl.ds(at + hop, 8), :]
            for tile in range(tiles - 1, -1, -1):
                at = 8 * tile
                sums[slot, h, pl.ds(at, 8), :] = twos[h, pl.ds(at, 8), :] + twos[h, pl.ds(at + 4, 8), :]

    def combine(low, here, high, out, side):
        for tile in range(tiles):
            rows = pl.ds(8 * tile, 8)
            outer, inner = beside([sums[here, h, rows, :] for h in range(halves)], lane)
            for h in range(halves):
                lanes = pl.ds(LANES * h, LANES)
                along_r = coef[0, h] * outer[h] + coef[1, h] * inner[h]
                across = sums[high, h, rows, :] - sums[low, h, rows, :]
                out_r[out, side, rows, lanes] = along_r + coef[3, h] * across
                out_phi[out, side, rows, lanes] = coef[2, h] * across - 0.3 * along_r

    integrate(0, 0)
    integrate(1, 1)

    def body(g, _):
        now = lax.rem(g, 2)
        new, old = 2 * now, 2 - 2 * now
        integrate(2 * g, new)
        integrate(2 * g + 1, new + 1)

        @pl.when(g >= 3)
        def _():
            for copy in out_copies(g - 3, now):
                copy.wait()

        combine(old, old + 1, new, now, 0)
        combine(old + 1, new, new + 1, now, 1)
        for copy in out_copies(g - 1, now):
            copy.start()
        return 0

    lax.fori_loop(1, pairs + 1, body, 0)
    for g in (pairs - 1, pairs):
        for copy in out_copies(g - 1, g % 2):
            copy.wait()
    for part in range(parts):
        pot_copy(part).wait()


def coefficients(radial, sectors):
    radius = radial * 0.5 + np.arange(radial, dtype=np.float64) + 0.5
    step_phi = 2.0 * math.pi / sectors
    around = 1.0 / (radius * step_phi) ** 2
    diag = 4.0 + 2.0 * around
    has_next = np.arange(radial) < radial - 1
    has_prev = np.arange(radial) > 0
    drift = 1.0 / (1.09 * 32.0)
    across = -0.5 * drift / (radius * step_phi)
    relax = [(1.0 + 0.5 / radius) * has_next, (1.0 - 0.5 / radius) * has_prev, around, RELAX / diag]
    shift = [-0.5 * drift * has_next, 0.5 * drift * has_prev, across, 0.3 * across]

    def tiled(rows):
        halves = np.stack(rows).astype(np.float32).reshape(len(rows), radial // LANES, 1, LANES)
        return jnp.asarray(np.ascontiguousarray(np.broadcast_to(halves, halves.shape[:2] + (8, LANES))))

    return tiled(relax), tiled(shift)


def local(slabs, rings, potential_in, charge, cell_kind):
    sectors, depth, radial = potential_in.shape
    pairs, halves = sectors // 2, radial // LANES
    tall = depth + 2 * PAD
    relax, shift = coefficients(radial, sectors * rings)
    any_spec = pl.BlockSpec(memory_space=pl.ANY)
    vmem_spec = pl.BlockSpec(memory_space=pltpu.VMEM)
    f32 = jnp.float32
    dma = pltpu.SemaphoreType.DMA
    full, carry = pl.pallas_call(
        functools.partial(relax_kernel, slabs, rings),
        out_shape=(
            pltpu.VMEM((sectors + 2, depth, radial), f32),
            pltpu.VMEM((halves, sectors + 2, LANES), f32),
        ),
        in_specs=[any_spec, any_spec, any_spec, vmem_spec],
        out_specs=(vmem_spec, vmem_spec),
        scratch_shapes=[
            pltpu.VMEM((sectors, depth, radial), f32),
            pltpu.VMEM((sectors, depth, radial), f32),
            pltpu.VMEM((sectors, depth, radial), jnp.int32),
            pltpu.VMEM((halves, pairs + 2, tall, LANES), f32),
            pltpu.VMEM((halves, pairs + 2 * PASSES, tall, LANES), f32),
            pltpu.VMEM((2, halves, pairs + 2, tall, LANES), f32),
            pltpu.VMEM((PASSES + 1, 2, halves, pairs, 2, LANES), f32),
            pltpu.VMEM((PASSES + 1, 2, halves, pairs, 2, LANES), f32),
            pltpu.VMEM((PASSES, 2, 2, halves, 2, LANES), f32),
            pltpu.VMEM((halves, sectors, LANES), f32),
            pltpu.VMEM((slabs - 1, halves, sectors, LANES), f32),
            pltpu.VMEM((2, halves, 1, LANES), f32),
            pltpu.VMEM((slabs - 1, 2, halves, 1, LANES), f32),
            dma((pairs + 2, 3)),
            dma((PASSES, 3, 2)),
            dma((PASSES, 3, 2)),
            dma((PASSES + 1, 2)),
            dma((PASSES + 1, 2)),
            dma((PASSES, 2, 2)),
            dma((PASSES, 2, 2)),
            dma((2,)),
            dma((2,)),
            dma((slabs - 1,)),
            dma((slabs - 1,)),
            dma((slabs - 1, 2)),
            dma((slabs - 1, 2)),
        ],
        compiler_params=pltpu.CompilerParams(
            collective_id=0, has_side_effects=True, vmem_limit_bytes=48 * 2**20
        ),
    )(potential_in, charge, cell_kind, relax)

    full = pltpu.with_memory_space_constraint(full, pltpu.VMEM)
    carry = pltpu.with_memory_space_constraint(carry, pltpu.VMEM)
    block = jax.ShapeDtypeStruct((sectors, depth, radial), f32)
    return pl.pallas_call(
        drift_kernel,
        out_shape=(block, block, block),
        in_specs=[vmem_spec, vmem_spec, vmem_spec],
        out_specs=(any_spec,) * 3,
        scratch_shapes=[
            pltpu.VMEM((halves, depth + 8, LANES), f32),
            pltpu.VMEM((halves, depth + 8, LANES), f32),
            pltpu.VMEM((halves, depth + 8, LANES), f32),
            pltpu.VMEM((4, halves, depth, LANES), f32),
            pltpu.VMEM((2, 2, depth, radial), f32),
            pltpu.VMEM((2, 2, depth, radial), f32),
            dma((4,)),
            dma((2, 2)),
        ],
        compiler_params=pltpu.CompilerParams(vmem_limit_bytes=16 * 2**20),
    )(shift, full, carry)


def solution(mesh):
    spec = P("phi", "gz", None)
    body = functools.partial(local, mesh.shape["gz"], mesh.shape["phi"])
    return jax.shard_map(body, mesh=mesh, in_specs=(spec,) * 3, out_specs=(spec,) * 3, check_vma=False)
```

time: 62.3 us -> 50.7 us (0.81)
  Pallas kernels: 61.1 us -> 49.1 us
  local copies, waits for them, and re-layouts: 0 us -> 0.76 us
    pallas_call x1, Pallas kernels: 45.9 us -> 39.6 us  [local(): pl.pallas_call(functools.partial(relax_kernel, slabs, rings), out_shape=(...]
    pallas_call x1, Pallas kernels: 15.2 us -> 9.48 us  [local(): pl.pallas_call(drift_kernel, out_shape=(block, block, block), in_specs=[v...]
    unnamed x0 -> x4, local copies, waits for them, and re-layouts: none -> 0.76 us
where the time goes in v1:
time: 50.7 us; the launch traced here: 50.5 us
  Pallas kernels  49.1 us (97%)
  local copies, waits for them, and re-layouts  0.76 us (1%)
  between operations  0.66 us (1%)
    pallas_call x1, Pallas kernels, local(): pl.pallas_call(functools.partial(relax_kernel, slabs, rings), out_shape=(...  39.6 us
    pallas_call x1, Pallas kernels, local(): pl.pallas_call(drift_kernel, out_shape=(block, block, block), in_specs=[v...  9.48 us

profile of v1, /device:TPU:0, one launch (start us, length us, event | category | flops | bytes accessed | tf_op | source)
XLA Modules:
  0.0 50.5 jit_solution(5300983790975782762)
XLA Ops:
  0.6 0.0 copy-start
  0.6 0.0 copy-start.1
  0.7 0.8 %copy-done.1 = f32[4,2,8,128]{3,2,1,0:T(8,128)S(1)} copy-done((f32[4,2,8,128]{3,2,1,0:T(8,128)S(1)}, f32[4,2,8,128]{3,2,1,0:T(8,128)}, u32[]{:S(2)}) %copy-start.1) | copy-done | bytes 32792
  1.4 39.6 %shard_map.76 = (f32[34,128,256]{2,1,0:T(8,128)S(1)}, f32[2,34,128]{2,1,0:T(8,128)S(1)}) custom-call(f32[32,128,256]{2,1,0:T(8,128)} %pot.1, f32[32,128,256]{2,1,0:T(8,128)} %chg.1, s32[32,128,256]{2,1,0:T(8,128)} %kind.1, f32[4,2,8,128]{3,2,1,0:T(8,128)S(1)} %copy-done.1), custom_call_target="tpu_custom_call" | custom-call | tf_op jit(solution)/shard_map/pallas_call | solution.py:500
  41.0 0.0 copy-done
  41.0 9.5 %shard_map.77 = (f32[32,128,256]{2,1,0:T(8,128)}, f32[32,128,256]{2,1,0:T(8,128)}, f32[32,128,256]{2,1,0:T(8,128)}) custom-call(f32[4,2,8,128]{3,2,1,0:T(8,128)S(1)} %copy-done, f32[34,128,256]{2,1,0:T(8,128)S(1)} %get-tuple-element.5.full, f32[2,34,128]{2,1,0:T(8,128)S(1)} %get-tuple-element.6.carry), custom_call_target="tpu_custom_call" | custom-call | tf_op jit(solution)/shard_map/pallas_call | solution.py:544
Async XLA Ops:
  0.6 40.4 %copy-start = (f32[4,2,8,128]{3,2,1,0:T(8,128)S(1)}, f32[4,2,8,128]{3,2,1,0:T(8,128)}, u32[]{:S(2)}) copy-start(f32[4,2,8,128]{3,2,1,0:T(8,128)} %constant.5.clone.coef) | copy-start | bytes 98308
  0.6 0.8 %copy-start.1 = (f32[4,2,8,128]{3,2,1,0:T(8,128)S(1)}, f32[4,2,8,128]{3,2,1,0:T(8,128)}, u32[]{:S(2)}) copy-start(f32[4,2,8,128]{3,2,1,0:T(8,128)} %constant.4.clone.coef) | copy-start | bytes 98308

commit v2 on v1

--- a/solution.py
+++ b/solution.py
@@ -3,7 +3,6 @@
 
 import jax
 import jax.numpy as jnp
-import numpy as np
 from jax import lax
 from jax.experimental import pallas as pl
 from jax.experimental.pallas import tpu as pltpu
@@ -16,6 +15,7 @@
 PAD = 16
 LANES = 128
 RED, BLACK = 0, 1
+UNROLL = 2
 
 
 def parity_mask():
@@ -33,9 +33,19 @@
     return outer, inner
 
 
+def geometry(half, radial, sectors):
+    cell = lax.broadcasted_iota(jnp.int32, (8, LANES), 1) + LANES * half
+    radius = radial * 0.5 + cell.astype(jnp.float32) + 0.5
+    step = radius * (2.0 * math.pi / sectors)
+    around = 1.0 / (step * step)
+    outward = jnp.where(cell < radial - 1, 1.0 + 0.5 / radius, 0.0)
+    inward = jnp.where(cell > 0, 1.0 - 0.5 / radius, 0.0)
+    return outward, inward, around, 4.0 + 2.0 * around, step
+
+
 def relax_kernel(
-    slabs, rings, pot, chg, kind, coef, full, carry,
-    pot_in, chg_in, kind_in, red, black, source, zsend, zrecv, crecv, total, total_recv, edge, edge_recv,
+    slabs, rings, pot, chg, kind, full, carry,
+    coef, pot_in, chg_in, kind_in, red, black, source, zsend, zrecv, crecv, total, total_recv, edge, edge_recv,
     load_sem, jsend_sem, jrecv_sem, zsend_sem, zrecv_sem, csend_sem, crecv_sem,
     fsend_sem, frecv_sem, tsend_sem, trecv_sem, esend_sem, erecv_sem,
 ):
@@ -83,6 +93,11 @@
         peer = lax.rem(slab + step, slabs)
         for column in (left, ring, right):
             pl.semaphore_signal(barrier, inc=1, device_id={"gz": peer, "phi": column}, device_id_type=MESH)
+
+    for h in range(halves):
+        outward, inward, around_i, diag, _ = geometry(h, radial, sectors * rings)
+        for n, values in enumerate((outward, inward, around_i, RELAX / diag)):
+            coef[n, h] = values
 
     nothing = jnp.zeros((8, LANES), jnp.float32)
     held = jnp.full((8, LANES), FIXED, jnp.float32)
@@ -227,8 +242,17 @@
             for copy in jcopies(exchange, side):
                 copy.start()
 
-    def loop(low, high, body):
-        lax.fori_loop(low, high, lambda p, _: (body(p), 0)[1], 0)
+    def loop(low, high, body, unroll=UNROLL):
+        odd = (high - low) % unroll
+
+        def several(n, _):
+            for step in range(unroll):
+                body(low + odd + n * unroll + step)
+            return 0
+
+        for p in range(low, low + odd):
+            body(p)
+        lax.fori_loop(0, (high - low) // unroll, several, 0)
 
     inside = range(1, tiles - 1)
     whole = range(tiles)
@@ -277,7 +301,7 @@
         arrive(p)
         red_inside(p - 1)
 
-    loop(2, pairs - 1, arrive_and_update)
+    loop(2, pairs - 1, arrive_and_update, 1)
     red_inside(pairs - 2)
 
     for sweep in range(PASSES):
@@ -383,10 +407,10 @@
 
 
 def drift_kernel(
-    coef, full, carry, potential, shift_r, shift_phi,
-    runs, ones, twos, sums, out_r, out_phi, pot_sem, out_sem,
+    rings, full, carry, potential, shift_r, shift_phi,
+    coef, runs, ones, twos, sums, out_r, out_phi, pot_sem, out_sem,
 ):
-    halves, tall = runs.shape[0], runs.shape[1]
+    halves = runs.shape[1]
     sectors = full.shape[0] - 2
     depth = full.shape[1]
     pairs = sectors // 2
@@ -394,105 +418,83 @@
     row = lax.broadcasted_iota(jnp.int32, (8, LANES), 0)
     lane = lax.broadcasted_iota(jnp.int32, (8, LANES), 1)
 
-    parts = pot_sem.shape[0]
-
-    def pot_copy(part):
-        count = sectors // parts
-        return pltpu.make_async_copy(
-            full.at[pl.ds(1 + part * count, count)], potential.at[pl.ds(part * count, count)], pot_sem.at[part]
-        )
-
-    def out_copies(pair, slot):
+    pot_copy = pltpu.make_async_copy(full.at[pl.ds(1, sectors)], potential, pot_sem)
+    pot_copy.start()
+    drift = 1.0 / (1.09 * 32.0)
+    for h in range(halves):
+        outward, inward, _, _, step = geometry(h, LANES * halves, sectors * rings)
+        coef[0, h] = jnp.where(outward > 0.0, -0.5 * drift, 0.0)
+        coef[1, h] = jnp.where(inward > 0.0, 0.5 * drift, 0.0)
+        coef[2, h] = -0.5 * drift / step
+        coef[3, h] = 0.3 * (-0.5 * drift / step)
+
+    def out_copies(pair):
         planes = pl.ds(2 * pair, 2)
         return [
-            pltpu.make_async_copy(out_r.at[slot], shift_r.at[planes], out_sem.at[slot, 0]),
-            pltpu.make_async_copy(out_phi.at[slot], shift_phi.at[planes], out_sem.at[slot, 1]),
+            pltpu.make_async_copy(src.at[planes], dst.at[planes], out_sem.at[n, pair])
+            for n, (src, dst) in enumerate(((out_r, shift_r), (out_phi, shift_phi)))
         ]
-
-    for part in range(parts):
-        pot_copy(part).start()
 
     def integrate(plane, slot):
         for h in range(halves):
             after = jnp.broadcast_to(carry[h, pl.ds(plane, 1), :], (8, LANES))
             run = jnp.where(row == 0, after, 0.0)
             for ref in (runs, ones, twos):
-                ref[h, pl.ds(depth, 8), :] = run
+                ref[slot, h, pl.ds(depth, 8), :] = run
             for tile in range(tiles - 1, -1, -1):
                 run = run + full[plane, pl.ds(8 * tile, 8), pl.ds(LANES * h, LANES)]
-                runs[h, pl.ds(8 * tile, 8), :] = run
+                runs[slot, h, pl.ds(8 * tile, 8), :] = run
         for h in range(halves):
             for src, dst, hop in ((runs, ones, 1), (ones, twos, 2)):
                 for tile in range(tiles - 1, -1, -1):
                     at = 8 * tile
-                    dst[h, pl.ds(at, 8), :] = src[h, pl.ds(at, 8), :] + src[h, pl.ds(at + hop, 8), :]
+                    dst[slot, h, pl.ds(at, 8), :] = src[slot, h, pl.ds(at, 8), :] + src[slot, h, pl.ds(at + hop, 8), :]
             for tile in range(tiles - 1, -1, -1):
                 at = 8 * tile
-                sums[slot, h, pl.ds(at, 8), :] = twos[h, pl.ds(at, 8), :] + twos[h, pl.ds(at + 4, 8), :]
-
-    def combine(low, here, high, out, side):
+                sums[plane, h, pl.ds(at, 8), :] = twos[slot, h, pl.ds(at, 8), :] + twos[slot, h, pl.ds(at + 4, 8), :]
+
+    def combine(plane):
         for tile in range(tiles):
             rows = pl.ds(8 * tile, 8)
-            outer, inner = beside([sums[here, h, rows, :] for h in range(halves)], lane)
+            outer, inner = beside([sums[plane, h, rows, :] for h in range(halves)], lane)
             for h in range(halves):
                 lanes = pl.ds(LANES * h, LANES)
                 along_r = coef[0, h] * outer[h] + coef[1, h] * inner[h]
-                across = sums[high, h, rows, :] - sums[low, h, rows, :]
-                out_r[out, side, rows, lanes] = along_r + coef[3, h] * across
-                out_phi[out, side, rows, lanes] = coef[2, h] * across - 0.3 * along_r
-
-    integrate(0, 0)
-    integrate(1, 1)
+                across = sums[plane + 1, h, rows, :] - sums[plane - 1, h, rows, :]
+                out_r[plane - 1, rows, lanes] = along_r + coef[3, h] * across
+                out_phi[plane - 1, rows, lanes] = coef[2, h] * across - 0.3 * along_r
+
+    def emit(pair):
+        combine(2 * pair + 1)
+        combine(2 * pair + 2)
+        for copy in out_copies(pair):
+            copy.start()
+
+    for plane in range(4):
+        integrate(plane, plane % 2)
 
     def body(g, _):
-        now = lax.rem(g, 2)
-        new, old = 2 * now, 2 - 2 * now
-        integrate(2 * g, new)
-        integrate(2 * g + 1, new + 1)
-
-        @pl.when(g >= 3)
-        def _():
-            for copy in out_copies(g - 3, now):
-                copy.wait()
-
-        combine(old, old + 1, new, now, 0)
-        combine(old + 1, new, new + 1, now, 1)
-        for copy in out_copies(g - 1, now):
-            copy.start()
+        integrate(2 * g, 0)
+        integrate(2 * g + 1, 1)
+        emit(g - 2)
         return 0
 
-    lax.fori_loop(1, pairs + 1, body, 0)
-    for g in (pairs - 1, pairs):
-        for copy in out_copies(g - 1, g % 2):
+    lax.fori_loop(2, pairs + 1, body, 0)
+    emit(pairs - 1)
+
+    def drain(pair, _):
+        for copy in out_copies(pair):
             copy.wait()
-    for part in range(parts):
-        pot_copy(part).wait()
-
-
-def coefficients(radial, sectors):
-    radius = radial * 0.5 + np.arange(radial, dtype=np.float64) + 0.5
-    step_phi = 2.0 * math.pi / sectors
-    around = 1.0 / (radius * step_phi) ** 2
-    diag = 4.0 + 2.0 * around
-    has_next = np.arange(radial) < radial - 1
-    has_prev = np.arange(radial) > 0
-    drift = 1.0 / (1.09 * 32.0)
-    across = -0.5 * drift / (radius * step_phi)
-    relax = [(1.0 + 0.5 / radius) * has_next, (1.0 - 0.5 / radius) * has_prev, around, RELAX / diag]
-    shift = [-0.5 * drift * has_next, 0.5 * drift * has_prev, across, 0.3 * across]
-
-    def tiled(rows):
-        halves = np.stack(rows).astype(np.float32).reshape(len(rows), radial // LANES, 1, LANES)
-        return jnp.asarray(np.ascontiguousarray(np.broadcast_to(halves, halves.shape[:2] + (8, LANES))))
-
-    return tiled(relax), tiled(shift)
+        return 0
+
+    lax.fori_loop(0, pairs, drain, 0)
+    pot_copy.wait()
 
 
 def local(slabs, rings, potential_in, charge, cell_kind):
     sectors, depth, radial = potential_in.shape
     pairs, halves = sectors // 2, radial // LANES
     tall = depth + 2 * PAD
-    relax, shift = coefficients(radial, sectors * rings)
     any_spec = pl.BlockSpec(memory_space=pl.ANY)
     vmem_spec = pl.BlockSpec(memory_space=pltpu.VMEM)
     f32 = jnp.float32
@@ -503,9 +505,10 @@
             pltpu.VMEM((sectors + 2, depth, radial), f32),
             pltpu.VMEM((halves, sectors + 2, LANES), f32),
         ),
-        in_specs=[any_spec, any_spec, any_spec, vmem_spec],
+        in_specs=[any_spec] * 3,
         out_specs=(vmem_spec, vmem_spec),
         scratch_shapes=[
+            pltpu.VMEM((4, halves, 8, LANES), f32),
             pltpu.VMEM((sectors, depth, radial), f32),
             pltpu.VMEM((sectors, depth, radial), f32),
             pltpu.VMEM((sectors, depth, radial), jnp.int32),
@@ -536,28 +539,29 @@
         compiler_params=pltpu.CompilerParams(
             collective_id=0, has_side_effects=True, vmem_limit_bytes=48 * 2**20
         ),
-    )(potential_in, charge, cell_kind, relax)
+    )(potential_in, charge, cell_kind)
 
     full = pltpu.with_memory_space_constraint(full, pltpu.VMEM)
     carry = pltpu.with_memory_space_constraint(carry, pltpu.VMEM)
     block = jax.ShapeDtypeStruct((sectors, depth, radial), f32)
     return pl.pallas_call(
-        drift_kernel,
+        functools.partial(drift_kernel, rings),
         out_shape=(block, block, block),
-        in_specs=[vmem_spec, vmem_spec, vmem_spec],
+        in_specs=[vmem_spec, vmem_spec],
         out_specs=(any_spec,) * 3,
         scratch_shapes=[
-            pltpu.VMEM((halves, depth + 8, LANES), f32),
-            pltpu.VMEM((halves, depth + 8, LANES), f32),
-            pltpu.VMEM((halves, depth + 8, LANES), f32),
-            pltpu.VMEM((4, halves, depth, LANES), f32),
-            pltpu.VMEM((2, 2, depth, radial), f32),
-            pltpu.VMEM((2, 2, depth, radial), f32),
-            dma((4,)),
-            dma((2, 2)),
+            pltpu.VMEM((4, halves, 8, LANES), f32),
+            pltpu.VMEM((2, halves, depth + 8, LANES), f32),
+            pltpu.VMEM((2, halves, depth + 8, LANES), f32),
+            pltpu.VMEM((2, halves, depth + 8, LANES), f32),
+            pltpu.VMEM((sectors + 2, halves, depth, LANES), f32),
+            pltpu.VMEM((sectors, depth, radial), f32),
+            pltpu.VMEM((sectors, depth, radial), f32),
+            dma,
+            dma((2, pairs)),
         ],
-        compiler_params=pltpu.CompilerParams(vmem_limit_bytes=16 * 2**20),
-    )(shift, full, carry)
+        compiler_params=pltpu.CompilerParams(vmem_limit_bytes=24 * 2**20),
+    )(full, carry)
 
 
 def solution(mesh):

time: 50.7 us -> 44.7 us (0.88)
  Pallas kernels: 49.1 us -> 43.9 us
  local copies, waits for them, and re-layouts: 0.76 us -> 0 us
    pallas_call x1, Pallas kernels: 9.48 us -> 6.06 us  [local(): pl.pallas_call(functools.partial(drift_kernel, rings), out_shape=(block,...]
    pallas_call x1, Pallas kernels: 39.6 us -> 37.8 us  [local(): pl.pallas_call(functools.partial(relax_kernel, slabs, rings), out_shape=(...]
    unnamed x4 -> x0, local copies, waits for them, and re-layouts: 0.76 us -> none
where the time goes in v2:
time: 44.7 us; the launch traced here: 44.5 us
  Pallas kernels  43.9 us (98%)
  between operations  0.64 us (1%)
    pallas_call x1, Pallas kernels, local(): pl.pallas_call(functools.partial(relax_kernel, slabs, rings), out_shape=(...  37.8 us
    pallas_call x1, Pallas kernels, local(): pl.pallas_call(functools.partial(drift_kernel, rings), out_shape=(block,...  6.06 us

profile of v2, /device:TPU:0, one launch (start us, length us, event | category | flops | bytes accessed | tf_op | source)
XLA Modules:
  0.0 44.5 jit_solution(18099753825909948559)
XLA Ops:
  0.6 37.8 %shard_map.58 = (f32[34,128,256]{2,1,0:T(8,128)S(1)}, f32[2,34,128]{2,1,0:T(8,128)S(1)}) custom-call(f32[32,128,256]{2,1,0:T(8,128)} %pot.1, f32[32,128,256]{2,1,0:T(8,128)} %chg.1, s32[32,128,256]{2,1,0:T(8,128)} %kind.1), custom_call_target="tpu_custom_call" | custom-call | tf_op jit(solution)/shard_map/pallas_call | solution.py:502
  38.5 6.1 %shard_map.59 = (f32[32,128,256]{2,1,0:T(8,128)}, f32[32,128,256]{2,1,0:T(8,128)}, f32[32,128,256]{2,1,0:T(8,128)}) custom-call(f32[34,128,256]{2,1,0:T(8,128)S(1)} %get-tuple-element.5.full, f32[2,34,128]{2,1,0:T(8,128)S(1)} %get-tuple-element.6.carry), custom_call_target="tpu_custom_call" | custom-call | tf_op jit(solution)/shard_map/pallas_call | solution.py:547

commit v3 on v2

--- a/solution.py
+++ b/solution.py
@@ -21,15 +21,15 @@
 def parity_mask():
     row = lax.broadcasted_iota(jnp.int32, (8, LANES), 0)
     lane = lax.broadcasted_iota(jnp.int32, (8, LANES), 1)
-    return (row + lane) % 2 == 0
+    return ((row + lane) & 1) == 0
 
 
 def beside(halves, lane):
     ahead = [pltpu.roll(x, LANES - 1, axis=1) for x in halves]
     behind = [pltpu.roll(x, 1, axis=1) for x in halves]
     last = len(halves) - 1
-    outer = [ahead[h] if h == last else jnp.where(lane == LANES - 1, ahead[h + 1], ahead[h]) for h in range(last + 1)]
-    inner = [behind[h] if h == 0 else jnp.where(lane == 0, behind[h - 1], behind[h]) for h in range(last + 1)]
+    outer = [ahead[h] if h == last else lax.select(lane == LANES - 1, ahead[h + 1], ahead[h]) for h in range(last + 1)]
+    inner = [behind[h] if h == 0 else lax.select(lane == 0, behind[h - 1], behind[h]) for h in range(last + 1)]
     return outer, inner
 
 
@@ -45,9 +45,10 @@
 
 def relax_kernel(
     slabs, rings, pot, chg, kind, full, carry,
-    coef, pot_in, chg_in, kind_in, red, black, source, zsend, zrecv, crecv, total, total_recv, edge, edge_recv,
+    coef, pot_in, chg_in, kind_in, red, black, source, mixed, zsend, zrecv, crecv,
+    partial, total, total_recv, edge, edge_recv,
     load_sem, jsend_sem, jrecv_sem, zsend_sem, zrecv_sem, csend_sem, crecv_sem,
-    fsend_sem, frecv_sem, tsend_sem, trecv_sem, esend_sem, erecv_sem,
+    tsend_sem, trecv_sem, esend_sem, erecv_sem,
 ):
     halves = red.shape[0]
     sectors, depth, radial = pot_in.shape
@@ -57,7 +58,6 @@
     ring = lax.axis_index("phi")
     right, left = lax.rem(ring + 1, rings), lax.rem(ring + rings - 1, rings)
     has_next, has_prev = slab < slabs - 1, slab > 0
-    whole_rows = pl.ds(PAD, depth)
     halo = (pairs, pairs + 1)
 
     def loads(slot, planes, rows):
@@ -101,13 +101,22 @@
 
     nothing = jnp.zeros((8, LANES), jnp.float32)
     held = jnp.full((8, LANES), FIXED, jnp.float32)
-    for h in range(halves):
-        for rows in (pl.ds(PAD - 8, 8), pl.ds(PAD + depth, 8)):
-            for p in range(black.shape[1]):
+
+    def clear(p, _):
+        for h in range(halves):
+            for rows in (pl.ds(PAD - 8, 8), pl.ds(PAD + depth, 8)):
                 black[h, p, rows, :] = nothing
-            for p in range(pairs):
+        return 0
+
+    def clear_own(p, _):
+        for h in range(halves):
+            for rows in (pl.ds(PAD - 8, 8), pl.ds(PAD + depth, 8)):
                 red[h, p, rows, :] = nothing
                 source[RED, h, p, rows, :] = held
+        return 0
+
+    lax.fori_loop(0, black.shape[1], clear, 0)
+    lax.fori_loop(0, pairs, clear_own, 0)
 
     def prepare(p, which):
         mask = parity_mask()
@@ -118,61 +127,96 @@
                 plane, charges = [], []
                 for side in range(2):
                     what = kind_in[2 * p + side, rows, lanes]
-                    plane.append(jnp.where(what == 1, 0.0, pot_in[2 * p + side, rows, lanes]))
-                    charges.append(jnp.where(what == 0, chg_in[2 * p + side, rows, lanes], FIXED))
-                red[h, p, out, :] = jnp.where(mask, plane[0], plane[1])
-                black[h, p, out, :] = jnp.where(mask, plane[1], plane[0])
-                source[RED, h, p, out, :] = jnp.where(mask, charges[0], charges[1])
-                source[BLACK, h, p, out, :] = jnp.where(mask, charges[1], charges[0])
-
-    def fresh_tile(color, p, near, before, after, tile):
+                    plane.append(lax.select(what == 1, nothing, pot_in[2 * p + side, rows, lanes]))
+                    charges.append(lax.select(what == 0, chg_in[2 * p + side, rows, lanes], held))
+                red[h, p, out, :] = lax.select(mask, plane[0], plane[1])
+                black[h, p, out, :] = lax.select(mask, plane[1], plane[0])
+                source[RED, h, p, out, :] = lax.select(mask, charges[0], charges[1])
+                source[BLACK, h, p, out, :] = lax.select(mask, charges[1], charges[0])
+
+    def fresh_tiles(color, p, near, before, after, which):
         own, other = (red, black) if color == RED else (black, red)
         mask = parity_mask()
         lane = lax.broadcasted_iota(jnp.int32, (8, LANES), 1)
         first, second = (before, after) if color == RED else (after, before)
-        at = PAD + 8 * tile
-        rows = pl.ds(at, 8)
-        here = [other[h, near, rows, :] for h in range(halves)]
-        outer, inner = beside(here, lane)
-        result = []
-        for h in range(halves):
-            around = here[h] + jnp.where(mask, other[h, first, rows, :], other[h, second, rows, :])
-            along = other[h, near, pl.ds(at - 1, 8), :] + other[h, near, pl.ds(at + 1, 8), :]
-            put = source[color, h, p, rows, :]
-            old = own[h, p, rows, :]
-            gathered = (put + along) + (coef[0, h] * outer[h] + coef[1, h] * inner[h]) + coef[2, h] * around
-            fresh = coef[3, h] * gathered - (RELAX - 1.0) * old
-            result.append((jnp.where(put < 0.5 * FIXED, fresh, old), here[h]))
-        return result
+        factor = [[coef[n, h] for n in range(4)] for h in range(halves)]
+        for tile in which:
+            at = PAD + 8 * tile
+            rows = pl.ds(at, 8)
+            here = [other[h, near, rows, :] for h in range(halves)]
+            outer, inner = beside(here, lane)
+            result = []
+            for h in range(halves):
+                out_c, in_c, around_c, scale = factor[h]
+                around = here[h] + lax.select(mask, other[h, first, rows, :], other[h, second, rows, :])
+                along = other[h, near, pl.ds(at - 1, 8), :] + other[h, near, pl.ds(at + 1, 8), :]
+                put = source[color, h, p, rows, :]
+                old = own[h, p, rows, :]
+                gathered = (put + along) + (out_c * outer[h] + in_c * inner[h]) + around_c * around
+                fresh = scale * gathered - (RELAX - 1.0) * old
+                result.append((lax.select(put < 0.5 * FIXED, fresh, old), here[h]))
+            yield tile, result
 
     def update(color, p, near, before, after, which):
         own = red if color == RED else black
-        for tile in which:
-            for h, (value, _) in enumerate(fresh_tile(color, p, near, before, after, tile)):
+        for tile, result in fresh_tiles(color, p, near, before, after, which):
+            for h, (value, _) in enumerate(result):
                 own[h, p, pl.ds(PAD + 8 * tile, 8), :] = value
 
     def halo_black(exchange):
         return pairs + 2 * exchange, pairs + 2 * exchange + 1
 
-    def jcopies(exchange, side):
-        edge_pair = (pairs - 1, 0)[side]
-        moves = [(black, (slice(None), edge_pair), (slice(None), halo_black(exchange)[side]))]
+    def first_tiles(exchange):
+        return tiles // 2 + 1 - exchange
+
+    def piece_tiles(exchange, piece):
+        cut = first_tiles(exchange)
+        return (0, cut) if piece == 0 else (cut, tiles)
+
+    def jcopies(exchange, side, piece):
+        low, high = piece_tiles(exchange, piece)
+        if exchange == PASSES:
+            rows = pl.ds(8 * low, 8 * (high - low))
+            moves = [(full.at[(sectors, 1)[side], rows], full.at[(0, sectors + 1)[side], rows])]
+        else:
+            rows = pl.ds(PAD + 8 * low, 8 * (high - low))
+            edge_pair = (pairs - 1, 0)[side]
+            moves = [(black.at[:, edge_pair, rows], black.at[:, halo_black(exchange)[side], rows])]
         if exchange == 0:
-            moves.append((red, (slice(None), edge_pair), (slice(None), halo[side])))
-            moves.append((source, (RED, slice(None), edge_pair), (RED, slice(None), halo[side])))
+            moves.append((mixed.at[side, :, pl.ds(8 * low, 8 * (high - low))], red.at[:, halo[side], rows]))
         return [
             pltpu.make_async_remote_copy(
-                src_ref=ref.at[(*src, whole_rows)],
-                dst_ref=ref.at[(*dst, whole_rows)],
-                send_sem=jsend_sem.at[exchange, n, side],
-                recv_sem=jrecv_sem.at[exchange, n, side],
+                src_ref=src,
+                dst_ref=dst,
+                send_sem=jsend_sem.at[exchange, n, side, piece],
+                recv_sem=jrecv_sem.at[exchange, n, side, piece],
                 device_id={"phi": (right, left)[side]},
                 device_id_type=MESH,
             )
-            for n, (ref, src, dst) in enumerate(moves)
+            for n, (src, dst) in enumerate(moves)
         ]
 
-    slots = (lambda exchange: (0, PASSES) if exchange == 0 else (exchange,))
+    def on_j(exchange, piece, act):
+        for side in range(2):
+            for copy in jcopies(exchange, side, piece):
+                act(copy)
+
+    def mix(side):
+        p = (pairs - 1, 0)[side]
+        mask = parity_mask()
+        for tile in range(tiles):
+            rows = pl.ds(PAD + 8 * tile, 8)
+            for h in range(halves):
+                values, charges = red[h, p, rows, :], pltpu.roll(source[RED, h, p, rows, :], 1, axis=1)
+                both = (charges, values) if side == 0 else (values, charges)
+                mixed[side, h, pl.ds(8 * tile, 8), :] = lax.select(mask, *both)
+
+    def unmix(piece):
+        for tile in range(*piece_tiles(0, piece)):
+            rows = pl.ds(PAD + 8 * tile, 8)
+            for side in range(2):
+                for h in range(halves):
+                    source[RED, h, halo[side], rows, :] = pltpu.roll(red[h, halo[side], rows, :], LANES - 1, axis=1)
 
     def zcopy(slot, side):
         return pltpu.make_async_remote_copy(
@@ -198,18 +242,19 @@
         )
 
     def zmoves(exchange, side):
-        return [zcopy(slot, side) for slot in slots(exchange)] + [ccopy(exchange, side, face) for face in range(2)]
-
-    def when_sides(exchange, gate, act):
+        rows = [zcopy(exchange, side)] + ([zcopy(PASSES, side)] if exchange == 0 else [])
+        return [ccopy(exchange, side, face) for face in range(2)] + rows
+
+    def on_z(exchange, act):
         for side in range(2):
-            @pl.when(gate[side])
+            @pl.when((has_next, has_prev)[side])
             def _():
                 for copy in zmoves(exchange, side):
                     act(copy)
 
     def send_z(exchange):
-        for h in range(halves):
-            for p in range(pairs):
+        def gather(p, _):
+            for h in range(halves):
                 zsend[exchange, 0, h, p] = black[h, p, pl.ds(PAD + depth - 2, 2), :]
                 zsend[exchange, 1, h, p] = black[h, p, pl.ds(PAD, 2), :]
                 if exchange == 0:
@@ -217,8 +262,8 @@
                         zsend[PASSES, side, h, p, pl.ds(0, 1), :] = red[h, p, pl.ds(at, 1), :]
                         zsend[PASSES, side, h, p, pl.ds(1, 1), :] = source[RED, h, p, pl.ds(at, 1), :]
 
-    def start_z(exchange):
-        when_sides(exchange, (has_next, has_prev), lambda copy: copy.start())
+        for p in range(pairs):
+            gather(p, 0)
 
     def take_z(exchange):
         for side in range(2):
@@ -237,11 +282,6 @@
                     for face in range(2):
                         black[h, halo_black(exchange)[face], two, :] = crecv[exchange, side, face, h]
 
-    def start_j(exchange):
-        for side in range(2):
-            for copy in jcopies(exchange, side):
-                copy.start()
-
     def loop(low, high, body, unroll=UNROLL):
         odd = (high - low) % unroll
 
@@ -255,40 +295,60 @@
         lax.fori_loop(0, (high - low) // unroll, several, 0)
 
     inside = range(1, tiles - 1)
-    whole = range(tiles)
+    core = range(2, tiles - 2)
     rims = (0, tiles - 1)
 
     def red_inside(p):
         update(RED, p, p, p - 1, p + 1, inside)
 
-    def red_edges(exchange):
-        low, high = halo_black(exchange)
-        take_z(exchange)
-        loop(1, pairs - 1, lambda p: update(RED, p, p, p - 1, p + 1, (-1, 0, tiles - 1, tiles)))
-        for side in range(2):
-            for copy in jcopies(exchange, side):
-                copy.wait_recv()
-            if exchange == 0:
-                for copy in jcopies(exchange, 1 - side):
-                    copy.wait_send()
+    def finish(p, before, after, which, first):
+        mask = parity_mask()
+        sums = [[nothing if first else partial[h, 2 * p + side] for side in range(2)] for h in range(halves)]
+        for tile, result in fresh_tiles(BLACK, p, p, before, after, which):
+            for h, (value, near) in enumerate(result):
+                for side in range(2):
+                    plane = lax.select(mask, near, value) if side == 0 else lax.select(mask, value, near)
+                    full[2 * p + 1 + side, pl.ds(8 * tile, 8), pl.ds(LANES * h, LANES)] = plane
+                    sums[h][side] = sums[h][side] + plane
+        for h in range(halves):
+            for side in range(2):
+                partial[h, 2 * p + side] = sums[h][side]
+
+    def edges(sweep, piece):
+        low, high = halo_black(sweep)
+        on_j(sweep, piece, lambda copy: copy.wait_recv())
+        if sweep == 0:
+            unmix(piece)
+        cut = first_tiles(sweep)
+        own_tiles = range(-1, cut) if piece == 0 else range(cut, tiles + 1)
+        halo_tiles = range(cut - 1) if piece == 0 else range(cut - 1, tiles)
         for side in range(2):
             p, before, after = ((0, low, 1), (pairs - 1, pairs - 2, high))[side]
-            update(RED, p, p, before, after, range(-1, tiles + 1))
+            update(RED, p, p, before, after, own_tiles)
             p, near, before, after = ((halo[0], low, low, 0), (halo[1], high, pairs - 1, high))[side]
-            update(RED, p, near, before, after, whole)
+            update(RED, p, near, before, after, halo_tiles)
+        for p, before, after in ((0, halo[0], 1), (pairs - 1, pairs - 2, halo[1])):
+            if sweep < PASSES - 1:
+                update(BLACK, p, p, before, after, halo_tiles)
+            else:
+                finish(p, before, after, halo_tiles, piece == 0)
+        on_j(sweep + 1, piece, lambda copy: copy.start())
 
     for batch in ends:
         for copy in batch:
             copy.wait()
     loop(0, pairs, lambda p: prepare(p, rims))
     send_z(0)
-    pl.semaphore_wait(barrier, 2 + 3 * (slabs - 1))
-    start_z(0)
     for p in (0, pairs - 1):
         for copy in pair_loads(p):
             copy.wait()
         prepare(p, inside)
-    start_j(0)
+    for side in range(2):
+        mix(side)
+    pl.semaphore_wait(barrier, 2 + 3 * (slabs - 1))
+    on_z(0, lambda copy: copy.start())
+    for piece in range(2):
+        on_j(0, piece, lambda copy: copy.start())
 
     def arrive(p):
         for copy in pair_loads(p):
@@ -305,51 +365,33 @@
     red_inside(pairs - 2)
 
     for sweep in range(PASSES):
-        if sweep > 0:
-            loop(1, pairs - 1, red_inside)
-        red_edges(sweep)
-        if sweep > 0:
-            for side in range(2):
-                for copy in jcopies(sweep, side):
-                    copy.wait_send()
+        take_z(sweep)
+        loop(1, pairs - 1, lambda p: update(RED, p, p, p - 1, p + 1, (-1, 0, tiles - 1, tiles)))
+        for piece in range(2):
+            on_j(sweep, piece, lambda copy: copy.wait_send())
+        for piece in range(2):
+            edges(sweep, piece)
         if sweep < PASSES - 1:
-            update(BLACK, 0, 0, halo[0], 1, whole)
-            update(BLACK, pairs - 1, pairs - 1, pairs - 2, halo[1], whole)
-            start_j(sweep + 1)
             loop(1, pairs - 1, lambda p: update(BLACK, p, p, p - 1, p + 1, rims))
             send_z(sweep + 1)
-            start_z(sweep + 1)
+            on_z(sweep + 1, lambda copy: copy.start())
             loop(1, pairs - 1, lambda p: update(BLACK, p, p, p - 1, p + 1, inside))
-
-    def finish(p, before, after):
-        mask = parity_mask()
-        sums = [[jnp.zeros((8, LANES), jnp.float32) for _ in range(2)] for _ in range(halves)]
-        for tile in whole:
-            rows = pl.ds(8 * tile, 8)
-            for h, (value, near) in enumerate(fresh_tile(BLACK, p, p, before, after, tile)):
-                for side in range(2):
-                    plane = jnp.where(mask, near, value) if side == 0 else jnp.where(mask, value, near)
-                    full[2 * p + 1 + side, rows, pl.ds(LANES * h, LANES)] = plane
-                    sums[h][side] = sums[h][side] + plane
-        for h in range(halves):
-            for side in range(2):
-                total[h, pl.ds(2 * p + side, 1), :] = jnp.sum(sums[h][side], axis=0, keepdims=True)
-
-    def fcopy(side):
-        return pltpu.make_async_remote_copy(
-            src_ref=full.at[(sectors, 1)[side]],
-            dst_ref=full.at[(0, sectors + 1)[side]],
-            send_sem=fsend_sem.at[side],
-            recv_sem=frecv_sem.at[side],
-            device_id={"phi": (right, left)[side]},
-            device_id_type=MESH,
-        )
-
-    finish(0, halo[0], 1)
-    finish(pairs - 1, pairs - 2, halo[1])
-    for side in range(2):
-        fcopy(side).start()
-    loop(1, pairs - 1, lambda p: finish(p, p - 1, p + 1))
+            on_z(sweep, lambda copy: copy.wait_send())
+            loop(1, pairs - 1, red_inside)
+        if sweep == PASSES - 2:
+            loop(2, pairs - 2, lambda p: finish(p, p - 1, p + 1, core, True))
+
+    for p in (1, pairs - 2):
+        finish(p, p - 1, p + 1, range(tiles), True)
+    loop(2, pairs - 2, lambda p: finish(p, p - 1, p + 1, (0, 1, tiles - 2, tiles - 1), False))
+
+    def add_up(group, _):
+        for n in range(8):
+            for h in range(halves):
+                total[h, pl.ds(8 * group + n, 1), :] = jnp.sum(partial[h, 8 * group + n], axis=0, keepdims=True)
+        return 0
+
+    lax.fori_loop(0, sectors // 8, add_up, 0)
     for h in range(halves):
         edge[0, h] = total[h, pl.ds(sectors - 1, 1), :]
         edge[1, h] = total[h, pl.ds(0, 1), :]
@@ -384,6 +426,7 @@
                 copy.start()
 
     carry[...] = jnp.zeros(carry.shape, jnp.float32)
+    on_z(PASSES - 1, lambda copy: copy.wait_send())
     for step in range(1, slabs):
         @pl.when(slab + step < slabs)
         def _():
@@ -394,16 +437,13 @@
                 for face, at in ((0, 0), (1, sectors + 1)):
                     carry[h, pl.ds(at, 1), :] = carry[h, pl.ds(at, 1), :] + edge_recv[step - 1, face, h]
 
-    for side in range(2):
-        fcopy(side).wait_recv()
-        fcopy(side).wait_send()
+    for piece in range(2):
+        on_j(PASSES, piece, lambda copy: copy.wait())
     for step in range(1, slabs):
         @pl.when(slab >= step)
         def _():
             for copy in tcopies(step):
                 copy.wait_send()
-    for sweep in range(PASSES):
-        when_sides(sweep, (has_next, has_prev), lambda copy: copy.wait_send())
 
 
 def drift_kernel(
@@ -515,22 +555,22 @@
             pltpu.VMEM((halves, pairs + 2, tall, LANES), f32),
             pltpu.VMEM((halves, pairs + 2 * PASSES, tall, LANES), f32),
             pltpu.VMEM((2, halves, pairs + 2, tall, LANES), f32),
+            pltpu.VMEM((2, halves, depth, LANES), f32),
             pltpu.VMEM((PASSES + 1, 2, halves, pairs, 2, LANES), f32),
             pltpu.VMEM((PASSES + 1, 2, halves, pairs, 2, LANES), f32),
             pltpu.VMEM((PASSES, 2, 2, halves, 2, LANES), f32),
+            pltpu.VMEM((halves, sectors, 8, LANES), f32),
             pltpu.VMEM((halves, sectors, LANES), f32),
             pltpu.VMEM((slabs - 1, halves, sectors, LANES), f32),
             pltpu.VMEM((2, halves, 1, LANES), f32),
             pltpu.VMEM((slabs - 1, 2, halves, 1, LANES), f32),
             dma((pairs + 2, 3)),
-            dma((PASSES, 3, 2)),
-            dma((PASSES, 3, 2)),
+            dma((PASSES + 1, 2, 2, 2)),
+            dma((PASSES + 1, 2, 2, 2)),
             dma((PASSES + 1, 2)),
             dma((PASSES + 1, 2)),
             dma((PASSES, 2, 2)),
             dma((PASSES, 2, 2)),
-            dma((2,)),
-            dma((2,)),
             dma((slabs - 1,)),
             dma((slabs - 1,)),
             dma((slabs - 1, 2)),

time: 44.7 us -> 40.4 us (0.904)
  Pallas kernels: 43.9 us -> 39.6 us
    pallas_call x1, Pallas kernels: 37.8 us -> 33.6 us  [local(): pl.pallas_call(functools.partial(relax_kernel, slabs, rings), out_shape=(...]
where the time goes in v3:
time: 40.4 us; the launch traced here: 40.2 us
  Pallas kernels  39.6 us (98%)
  between operations  0.64 us (2%)
    pallas_call x1, Pallas kernels, local(): pl.pallas_call(functools.partial(relax_kernel, slabs, rings), out_shape=(...  33.6 us
    pallas_call x1, Pallas kernels, local(): pl.pallas_call(functools.partial(drift_kernel, rings), out_shape=(block,...  6.06 us

profile of v3, /device:TPU:0, one launch (start us, length us, event | category | flops | bytes accessed | tf_op | source)
XLA Modules:
  0.0 40.2 jit_solution(17727424982118700299)
XLA Ops:
  0.6 33.6 %shard_map.58 = (f32[34,128,256]{2,1,0:T(8,128)S(1)}, f32[2,34,128]{2,1,0:T(8,128)S(1)}) custom-call(f32[32,128,256]{2,1,0:T(8,128)} %pot.1, f32[32,128,256]{2,1,0:T(8,128)} %chg.1, s32[32,128,256]{2,1,0:T(8,128)} %kind.1), custom_call_target="tpu_custom_call" | custom-call | tf_op jit(solution)/shard_map/pallas_call | solution.py:542
  34.2 6.1 %shard_map.59 = (f32[32,128,256]{2,1,0:T(8,128)}, f32[32,128,256]{2,1,0:T(8,128)}, f32[32,128,256]{2,1,0:T(8,128)}) custom-call(f32[34,128,256]{2,1,0:T(8,128)S(1)} %get-tuple-element.5.full, f32[2,34,128]{2,1,0:T(8,128)S(1)} %get-tuple-element.6.carry), custom_call_target="tpu_custom_call" | custom-call | tf_op jit(solution)/shard_map/pallas_call | solution.py:587

commit v4 on v3

--- a/solution.py
+++ b/solution.py
@@ -166,24 +166,24 @@
     def halo_black(exchange):
         return pairs + 2 * exchange, pairs + 2 * exchange + 1
 
-    def first_tiles(exchange):
-        return tiles // 2 + 1 - exchange
-
-    def piece_tiles(exchange, piece):
-        cut = first_tiles(exchange)
-        return (0, cut) if piece == 0 else (cut, tiles)
+    def outer_tiles(exchange):
+        return tiles // 4 + 2 - exchange
+
+    def spans(cut, piece):
+        return [(0, cut), (tiles - cut, tiles)] if piece == 0 else [(cut, tiles - cut)]
 
     def jcopies(exchange, side, piece):
-        low, high = piece_tiles(exchange, piece)
-        if exchange == PASSES:
-            rows = pl.ds(8 * low, 8 * (high - low))
-            moves = [(full.at[(sectors, 1)[side], rows], full.at[(0, sectors + 1)[side], rows])]
-        else:
+        moves = []
+        for low, high in spans(outer_tiles(exchange), piece):
+            plain = pl.ds(8 * low, 8 * (high - low))
             rows = pl.ds(PAD + 8 * low, 8 * (high - low))
+            if exchange == PASSES:
+                moves.append((full.at[(sectors, 1)[side], plain], full.at[(0, sectors + 1)[side], plain]))
+                continue
             edge_pair = (pairs - 1, 0)[side]
-            moves = [(black.at[:, edge_pair, rows], black.at[:, halo_black(exchange)[side], rows])]
-        if exchange == 0:
-            moves.append((mixed.at[side, :, pl.ds(8 * low, 8 * (high - low))], red.at[:, halo[side], rows]))
+            moves.append((black.at[:, edge_pair, rows], black.at[:, halo_black(exchange)[side], rows]))
+            if exchange == 0:
+                moves.append((mixed.at[side, :, plain], red.at[:, halo[side], rows]))
         return [
             pltpu.make_async_remote_copy(
                 src_ref=src,
@@ -212,11 +212,12 @@
                 mixed[side, h, pl.ds(8 * tile, 8), :] = lax.select(mask, *both)
 
     def unmix(piece):
-        for tile in range(*piece_tiles(0, piece)):
-            rows = pl.ds(PAD + 8 * tile, 8)
-            for side in range(2):
-                for h in range(halves):
-                    source[RED, h, halo[side], rows, :] = pltpu.roll(red[h, halo[side], rows, :], LANES - 1, axis=1)
+        for low, high in spans(outer_tiles(0), piece):
+            for tile in range(low, high):
+                rows = pl.ds(PAD + 8 * tile, 8)
+                for side in range(2):
+                    for h in range(halves):
+                        source[RED, h, halo[side], rows, :] = pltpu.roll(red[h, halo[side], rows, :], LANES - 1, axis=1)
 
     def zcopy(slot, side):
         return pltpu.make_async_remote_copy(
@@ -283,7 +284,7 @@
                         black[h, halo_black(exchange)[face], two, :] = crecv[exchange, side, face, h]
 
     def loop(low, high, body, unroll=UNROLL):
-        odd = (high - low) % unroll
+        odd = (high - low) % unroll if unroll < high - low else high - low
 
         def several(n, _):
             for step in range(unroll):
@@ -292,7 +293,8 @@
 
         for p in range(low, low + odd):
             body(p)
-        lax.fori_loop(0, (high - low) // unroll, several, 0)
+        if odd < high - low:
+            lax.fori_loop(0, (high - low) // unroll, several, 0)
 
     inside = range(1, tiles - 1)
     core = range(2, tiles - 2)
@@ -319,9 +321,11 @@
         on_j(sweep, piece, lambda copy: copy.wait_recv())
         if sweep == 0:
             unmix(piece)
-        cut = first_tiles(sweep)
-        own_tiles = range(-1, cut) if piece == 0 else range(cut, tiles + 1)
-        halo_tiles = range(cut - 1) if piece == 0 else range(cut - 1, tiles)
+        cut = outer_tiles(sweep)
+        halo_tiles = [tile for low, high in spans(cut - 1, piece) for tile in range(low, high)]
+        own_tiles = [tile for low, high in spans(cut, piece) for tile in range(low, high)]
+        if piece == 0:
+            own_tiles = [-1, *own_tiles, tiles]
         for side in range(2):
             p, before, after = ((0, low, 1), (pairs - 1, pairs - 2, high))[side]
             update(RED, p, p, before, after, own_tiles)
@@ -364,17 +368,25 @@
     loop(2, pairs - 1, arrive_and_update, 1)
     red_inside(pairs - 2)
 
+    def black_rims(p):
+        update(BLACK, p, p, p - 1, p + 1, rims)
+
     for sweep in range(PASSES):
+        more = sweep < PASSES - 1
         take_z(sweep)
-        loop(1, pairs - 1, lambda p: update(RED, p, p, p - 1, p + 1, (-1, 0, tiles - 1, tiles)))
+        loop(1, pairs - 1, lambda p: update(RED, p, p, p - 1, p + 1, (-1, 0, tiles - 1, tiles)), pairs - 2)
+        if more:
+            loop(2, pairs - 2, black_rims, pairs - 4)
         for piece in range(2):
             on_j(sweep, piece, lambda copy: copy.wait_send())
-        for piece in range(2):
-            edges(sweep, piece)
-        if sweep < PASSES - 1:
-            loop(1, pairs - 1, lambda p: update(BLACK, p, p, p - 1, p + 1, rims))
+        edges(sweep, 0)
+        if more:
+            for p in (1, pairs - 2):
+                black_rims(p)
             send_z(sweep + 1)
             on_z(sweep + 1, lambda copy: copy.start())
+        edges(sweep, 1)
+        if more:
             loop(1, pairs - 1, lambda p: update(BLACK, p, p, p - 1, p + 1, inside))
             on_z(sweep, lambda copy: copy.wait_send())
             loop(1, pairs - 1, red_inside)
@@ -383,7 +395,7 @@
 
     for p in (1, pairs - 2):
         finish(p, p - 1, p + 1, range(tiles), True)
-    loop(2, pairs - 2, lambda p: finish(p, p - 1, p + 1, (0, 1, tiles - 2, tiles - 1), False))
+    loop(2, pairs - 2, lambda p: finish(p, p - 1, p + 1, (0, 1, tiles - 2, tiles - 1), False), pairs - 4)
 
     def add_up(group, _):
         for n in range(8):
@@ -565,8 +577,8 @@
             pltpu.VMEM((2, halves, 1, LANES), f32),
             pltpu.VMEM((slabs - 1, 2, halves, 1, LANES), f32),
             dma((pairs + 2, 3)),
-            dma((PASSES + 1, 2, 2, 2)),
-            dma((PASSES + 1, 2, 2, 2)),
+            dma((PASSES + 1, 4, 2, 2)),
+            dma((PASSES + 1, 4, 2, 2)),
             dma((PASSES + 1, 2)),
             dma((PASSES + 1, 2)),
             dma((PASSES, 2, 2)),

time: 40.4 us -> 38.5 us (0.953)
  Pallas kernels: 39.6 us -> 37.8 us
    pallas_call x1, Pallas kernels: 33.6 us -> 31.7 us  [local(): pl.pallas_call(functools.partial(relax_kernel, slabs, rings), out_shape=(...]
where the time goes in v4:
time: 38.5 us; the launch traced here: 38.4 us
  Pallas kernels  37.8 us (98%)
  between operations  0.64 us (2%)
    pallas_call x1, Pallas kernels, local(): pl.pallas_call(functools.partial(relax_kernel, slabs, rings), out_shape=(...  31.7 us
    pallas_call x1, Pallas kernels, local(): pl.pallas_call(functools.partial(drift_kernel, rings), out_shape=(block,...  6.06 us

profile of v4, /device:TPU:0, one launch (start us, length us, event | category | flops | bytes accessed | tf_op | source)
XLA Modules:
  0.0 38.4 jit_solution(6815289901851560839)
XLA Ops:
  0.6 31.7 %shard_map.58 = (f32[34,128,256]{2,1,0:T(8,128)S(1)}, f32[2,34,128]{2,1,0:T(8,128)S(1)}) custom-call(f32[32,128,256]{2,1,0:T(8,128)} %pot.1, f32[32,128,256]{2,1,0:T(8,128)} %chg.1, s32[32,128,256]{2,1,0:T(8,128)} %kind.1), custom_call_target="tpu_custom_call" | custom-call | tf_op jit(solution)/shard_map/pallas_call | solution.py:554
  32.3 6.1 %shard_map.59 = (f32[32,128,256]{2,1,0:T(8,128)}, f32[32,128,256]{2,1,0:T(8,128)}, f32[32,128,256]{2,1,0:T(8,128)}) custom-call(f32[34,128,256]{2,1,0:T(8,128)S(1)} %get-tuple-element.5.full, f32[2,34,128]{2,1,0:T(8,128)S(1)} %get-tuple-element.6.carry), custom_call_target="tpu_custom_call" | custom-call | tf_op jit(solution)/shard_map/pallas_call | solution.py:599

commit v5 on v4

--- a/solution.py
+++ b/solution.py
@@ -16,6 +16,7 @@
 LANES = 128
 RED, BLACK = 0, 1
 UNROLL = 2
+STEPS = 3
 
 
 def parity_mask():
@@ -167,7 +168,7 @@
         return pairs + 2 * exchange, pairs + 2 * exchange + 1
 
     def outer_tiles(exchange):
-        return tiles // 4 + 2 - exchange
+        return tiles // 4 + 1 - exchange
 
     def spans(cut, piece):
         return [(0, cut), (tiles - cut, tiles)] if piece == 0 else [(cut, tiles - cut)]
@@ -525,13 +526,19 @@
     for plane in range(4):
         integrate(plane, plane % 2)
 
-    def body(g, _):
-        integrate(2 * g, 0)
-        integrate(2 * g + 1, 1)
+    def step(g, slot):
+        integrate(2 * g, slot)
+        integrate(2 * g + 1, slot + 1)
         emit(g - 2)
+
+    group = STEPS if (pairs - 1) % STEPS == 0 else 1
+
+    def body(n, _):
+        for turn in range(group):
+            step(2 + n * group + turn, 2 * (turn % 2))
         return 0
 
-    lax.fori_loop(2, pairs + 1, body, 0)
+    lax.fori_loop(0, (pairs - 1) // group, body, 0)
     emit(pairs - 1)
 
     def drain(pair, _):
@@ -603,9 +610,9 @@
         out_specs=(any_spec,) * 3,
         scratch_shapes=[
             pltpu.VMEM((4, halves, 8, LANES), f32),
-            pltpu.VMEM((2, halves, depth + 8, LANES), f32),
-            pltpu.VMEM((2, halves, depth + 8, LANES), f32),
-            pltpu.VMEM((2, halves, depth + 8, LANES), f32),
+            pltpu.VMEM((4, halves, depth + 8, LANES), f32),
+            pltpu.VMEM((4, halves, depth + 8, LANES), f32),
+            pltpu.VMEM((4, halves, depth + 8, LANES), f32),
             pltpu.VMEM((sectors + 2, halves, depth, LANES), f32),
             pltpu.VMEM((sectors, depth, radial), f32),
             pltpu.VMEM((sectors, depth, radial), f32),

time: 38.5 us -> 37 us (0.961)
  Pallas kernels: 37.8 us -> 36.2 us
    pallas_call x1, Pallas kernels: 6.06 us -> 4.81 us  [local(): pl.pallas_call(functools.partial(drift_kernel, rings), out_shape=(block,...]
where the time goes in v5:
time: 37 us; the launch traced here: 36.8 us
  Pallas kernels  36.2 us (98%)
  between operations  0.64 us (2%)
    pallas_call x1, Pallas kernels, local(): pl.pallas_call(functools.partial(relax_kernel, slabs, rings), out_shape=(...  31.4 us
    pallas_call x1, Pallas kernels, local(): pl.pallas_call(functools.partial(drift_kernel, rings), out_shape=(block,...  4.81 us

profile of v5, /device:TPU:0, one launch (start us, length us, event | category | flops | bytes accessed | tf_op | source)
XLA Modules:
  0.0 36.8 jit_solution(12163987449906217983)
XLA Ops:
  0.6 31.4 %shard_map.58 = (f32[34,128,256]{2,1,0:T(8,128)S(1)}, f32[2,34,128]{2,1,0:T(8,128)S(1)}) custom-call(f32[32,128,256]{2,1,0:T(8,128)} %pot.1, f32[32,128,256]{2,1,0:T(8,128)} %chg.1, s32[32,128,256]{2,1,0:T(8,128)} %kind.1), custom_call_target="tpu_custom_call" | custom-call | tf_op jit(solution)/shard_map/pallas_call | solution.py:561
  32.0 4.8 %shard_map.59 = (f32[32,128,256]{2,1,0:T(8,128)}, f32[32,128,256]{2,1,0:T(8,128)}, f32[32,128,256]{2,1,0:T(8,128)}) custom-call(f32[34,128,256]{2,1,0:T(8,128)S(1)} %get-tuple-element.5.full, f32[2,34,128]{2,1,0:T(8,128)S(1)} %get-tuple-element.6.carry), custom_call_target="tpu_custom_call" | custom-call | tf_op jit(solution)/shard_map/pallas_call | solution.py:606

commit v6 on v5

--- a/solution.py
+++ b/solution.py
@@ -168,7 +168,7 @@
         return pairs + 2 * exchange, pairs + 2 * exchange + 1
 
     def outer_tiles(exchange):
-        return tiles // 4 + 1 - exchange
+        return tiles // 4 - exchange
 
     def spans(cut, piece):
         return [(0, cut), (tiles - cut, tiles)] if piece == 0 else [(cut, tiles - cut)]
@@ -351,9 +351,9 @@
     for side in range(2):
         mix(side)
     pl.semaphore_wait(barrier, 2 + 3 * (slabs - 1))
-    on_z(0, lambda copy: copy.start())
     for piece in range(2):
         on_j(0, piece, lambda copy: copy.start())
+    on_z(0, lambda copy: copy.start())
 
     def arrive(p):
         for copy in pair_loads(p):

time: 37 us -> 39.6 us (1.070)
  Pallas kernels: 36.2 us -> 38.8 us
    pallas_call x1, Pallas kernels: 31.4 us -> 34 us  [local(): pl.pallas_call(functools.partial(relax_kernel, slabs, rings), out_shape=(...]
where the time goes in v6:
time: 39.6 us; the launch traced here: 39.4 us
  Pallas kernels  38.8 us (98%)
  between operations  0.64 us (2%)
    pallas_call x1, Pallas kernels, local(): pl.pallas_call(functools.partial(relax_kernel, slabs, rings), out_shape=(...  34 us
    pallas_call x1, Pallas kernels, local(): pl.pallas_call(functools.partial(drift_kernel, rings), out_shape=(block,...  4.81 us

profile of v6, /device:TPU:0, one launch (start us, length us, event | category | flops | bytes accessed | tf_op | source)
XLA Modules:
  0.0 39.4 jit_solution(1143663213852785196)
XLA Ops:
  0.6 34.0 %shard_map.58 = (f32[34,128,256]{2,1,0:T(8,128)S(1)}, f32[2,34,128]{2,1,0:T(8,128)S(1)}) custom-call(f32[32,128,256]{2,1,0:T(8,128)} %pot.1, f32[32,128,256]{2,1,0:T(8,128)} %chg.1, s32[32,128,256]{2,1,0:T(8,128)} %kind.1), custom_call_target="tpu_custom_call" | custom-call | tf_op jit(solution)/shard_map/pallas_call | solution.py:561
  34.6 4.8 %shard_map.59 = (f32[32,128,256]{2,1,0:T(8,128)}, f32[32,128,256]{2,1,0:T(8,128)}, f32[32,128,256]{2,1,0:T(8,128)}) custom-call(f32[34,128,256]{2,1,0:T(8,128)S(1)} %get-tuple-element.5.full, f32[2,34,128]{2,1,0:T(8,128)S(1)} %get-tuple-element.6.carry), custom_call_target="tpu_custom_call" | custom-call | tf_op jit(solution)/shard_map/pallas_call | solution.py:606
